TPU v7x, 512 devices: a whole 4x8x8 slice. The times are simulated.
512 devices in a mesh: dom: 64 (over z, x, core), col: 8 (over y).
Axes of the slice: x: 4, y: 8, z: 8, core: 2. Of those that a mesh axis runs over, the one named last changes fastest.
Arguments:
- feature: bfloat16 [32768, 1024], P('dom', 'col'), may hold values from -6 to 6
- cotangent: bfloat16 [32768, 1024], P('dom', 'col'), may hold values from -6 to 6
- node_type: int32 [32768], P('dom'), may hold values from 0 to 2
- self_gain: float32 [3, 1024], P(None, 'col'), may hold values from 0.1 to 1.9
- weights: bfloat16 [8, 1024, 1024], P(None, 'dom', 'col'), may hold values from -0.1875 to 0.1875
- tile_values: bfloat16 [2048, 128, 128], P('dom'), may hold values from -0.5 to 0.5
- tile_rel: int32 [2048], P('dom'), may hold values from 0 to 7
- tile_src: int32 [2048], P('dom'), may hold values from 0 to 3
- tile_peer: int32 [2048], P('dom'), may hold values from 0 to 63, as said below
- tile_count: int32 [64], P('dom'), may hold values from 24 to 32, as said below
- send_block: int32 [64, 64], P('dom'), may hold values from -1 to 3, as said below
Outputs:
- feature_grad: bfloat16 [32768, 1024], P('dom', 'col')
- weight_grad: bfloat16 [8, 1024, 1024], P(None, None, 'col')
Inputs may be any that keep to these rules, and one draw needn't show every extreme that they name: Slots 0 to tile_count - 1 of each partition hold its tiles, the others hold none; some partition uses all 32 slots in every draw. `tile_peer`: the used slots of one partition name distinct owner partitions. send_block[o, p] is at least 0 exactly when some used slot of partition p names o, and then it is that slot's destination block within o.
All inputs are finite; a program needn't handle non-finite values.
Results may differ from a plain program's by a relative error of at most 0.0052.
Values may be sent and summed in bfloat16 or wider, within the bound.
No kernel may reach another device: no remote copies, remote signals or barrier semaphores. Data moves between devices by JAX's collectives and lax.ppermute only.
A program may use at most 64 MiB of HBM per device.

v0:
```python
import math

import jax
import jax.numpy as jnp
from jax import lax
from jax.sharding import PartitionSpec as P


def body(
    feature,
    cotangent,
    node_type,
    self_gain,
    weights,
    tile_values,
    tile_rel,
    tile_src,
    tile_peer,
    tile_count,
    send_block,
):
    partitions = lax.axis_size("dom")
    row_count, col_width = cotangent.shape
    tile_size = tile_values.shape[1]
    block_count = row_count // tile_size
    relations = weights.shape[0]
    slot_count = tile_values.shape[0]
    type_count = self_gain.shape[0]
    grad_blocks = cotangent.reshape(block_count, tile_size, col_width)
    wanted = send_block[0]
    chooser = (wanted[:, None] == jnp.arange(block_count, dtype=jnp.int32)[None, :]).astype(
        jnp.bfloat16
    )
    outgoing = jnp.einsum(
        "pb,btk->ptk", chooser, grad_blocks, preferred_element_type=jnp.float32
    ).astype(jnp.bfloat16)
    incoming = lax.all_to_all(outgoing, "dom", split_axis=0, concat_axis=0, tiled=True)
    picked = jnp.take(incoming, tile_peer, axis=0)
    contribs = jnp.einsum("tds,tdk->tsk", tile_values, picked, preferred_element_type=jnp.float32)
    is_used = jnp.arange(slot_count, dtype=jnp.int32) < tile_count[0]
    slot_of = tile_rel * block_count + tile_src
    slot_table = (
        (slot_of[None, :] == jnp.arange(relations * block_count, dtype=jnp.int32)[:, None])
        & is_used[None, :]
    ).astype(jnp.float32)
    merged = jnp.einsum("mt,tsk->msk", slot_table, contribs, precision=lax.Precision.HIGHEST)
    block_grad = merged.astype(jnp.bfloat16).reshape(relations, row_count, col_width)
    kind_table = (node_type[:, None] == jnp.arange(type_count, dtype=jnp.int32)[None, :]).astype(
        jnp.float32
    )
    self_gains = jnp.dot(kind_table, self_gain, precision=lax.Precision.HIGHEST)
    self_term = cotangent.astype(jnp.float32) * self_gains
    weight_full = lax.all_gather(weights, "dom", axis=1, tiled=True)
    weight_cols = lax.all_to_all(weight_full, "col", split_axis=1, concat_axis=2, tiled=True)
    aggregated = jnp.einsum(
        "rnk,rjk->nj",
        lax.all_gather(block_grad, "col", axis=2, tiled=True),
        weight_cols,
        preferred_element_type=jnp.float32,
    )
    feature_grad = (aggregated + self_term).astype(jnp.bfloat16)
    weight_terms = jnp.einsum(
        "nj,rnk->rjk",
        lax.all_gather(feature, "col", axis=1, tiled=True),
        block_grad,
        preferred_element_type=jnp.float32,
    )
    norm_scale = 1.0 / math.sqrt(row_count * partitions)
    summed = lax.psum(weight_terms, "dom")
    weight_grad = (summed * norm_scale).astype(jnp.bfloat16)
    return (feature_grad, weight_grad)


def solution(mesh):
    return jax.shard_map(
        body,
        mesh=mesh,
        in_specs=(
            P("dom", "col"),
            P("dom", "col"),
            P("dom"),
            P(None, "col"),
            P(None, "dom", "col"),
            P("dom", None, None),
            P("dom"),
            P("dom"),
            P("dom"),
            P("dom"),
            P("dom", None),
        ),
        out_specs=(P("dom", "col"), P(None, None, "col")),
        check_vma=False,
    )
```

profile of v0, /device:TPU:1, one launch (start us, length us, event | category | flops | bytes accessed | tf_op | source)
XLA Modules:
  0.0 468.0 jit_solution(14236573666321858946)
XLA Ops:
  7.2 0.7 all-gather.8.cloned.1.call-update
  7.9 1.7 convolution_convert_fusion
  9.6 2.7 copy.38
  12.3 15.0 %all-to-all-start = ((bf16[64,128,128]{2,1,0:T(8,128)(2,1)}), bf16[64,128,128]{2,1,0:T(8,128)(2,1)S(1)}, u32[]{:S(2)}, u32[]{:S(2)}) async-start(bf16[64,128,128]{2,1,0:T(8,128)(2,1)} %copy.38), calls=%async_computation | async-start | bytes 4194304 | tf_op jit(solution)/shard_map/all_to_all | solution.py:37
  27.3 0.6 copy.42
  28.0 0.1 all-gather.6.cloned.1.call-update
  28.8 48.1 %all-to-all-done = bf16[64,128,128]{2,1,0:T(8,128)(2,1)S(1)} async-done(((bf16[64,128,128]{2,1,0:T(8,128)(2,1)}), bf16[64,128,128]{2,1,0:T(8,128)(2,1)S(1)}, u32[]{:S(2)}, u32[]{:S(2)}) %all-to-all-start) | async-done | bytes 2097184 | tf_op jit(solution)/shard_map/all_to_all | solution.py:37
  77.0 1.7 gather_fusion
  78.6 3.1 convolution_bitcast_fusion.1
  81.8 2.4 copy.40
  84.2 1.1 convolution_convert_fusion.1
  85.3 0.4 copy.41
  85.8 4.8 %convolution_bitcast_fusion = f32[8,1024,128]{1,2,0:T(8,128)} fusion(bf16[8,512,128]{2,1,0:T(8,128)(2,1)S(1)} %bitcast.32, bf16[512,1024]{1,0:T(8,128)(2,1)} %all-gather.8.cloned.1.call-done), kind=kOutput, calls=%fused_computation.2 | convolution fusion | flops 1073741824 | bytes 6291456 | tf_op jit(solution)/shard_map/nj,rnk->rjk/dot_general | solution.py:62
  90.7 0.5 all-gather.4.cloned.1.call-update
  91.2 53.5 %all-gather.6.cloned.1.call-done = bf16[8,1024,128]{2,0,1:T(8,128)(2,1)} async-done(((bf16[8,16,128]{2,0,1:T(8,128)(2,1)}), bf16[8,1024,128]{2,0,1:T(8,128)(2,1)}) %all-gather.6.cloned.1.call-update) | async-done | bytes 2097168 | tf_op jit(solution)/shard_map/all_gather | solution.py:53
  144.7 6.5 %all-to-all-start.1 = ((bf16[8,1024,128]{2,0,1:T(8,128)(2,1)}), bf16[8,1024,128]{2,0,1:T(8,128)(2,1)}, u32[]{:S(2)}, u32[]{:S(2)}) async-start(bf16[8,1024,128]{2,0,1:T(8,128)(2,1)} %all-gather.6.cloned.1.call-done), calls=%async_computation.1 | async-start | bytes 4194304 | tf_op jit(solution)/shard_map/all_to_all | solution.py:54
  151.2 200.6 %all-reduce.2.cloned.1.call-done = f32[8,1024,128]{1,2,0:T(8,128)} async-done(((f32[8,1024,128]{1,2,0:T(8,128)}), f32[8,1024,128]{1,2,0:T(8,128)}) %all-reduce.2.cloned.1.call-update) | async-done | bytes 4194320 | tf_op jit(solution)/shard_map/psum | solution.py:69
  351.8 2.8 multiply_convert_fusion
  354.6 2.4 copy.45
  357.0 2.9 copy.51
  359.9 2.4 all_to_all.20
  362.3 91.8 %all-gather.4.cloned.1.call-done = bf16[8,512,1024]{2,1,0:T(8,128)(2,1)} async-done(((bf16[8,512,128]{2,1,0:T(8,128)(2,1)}), bf16[8,512,1024]{2,1,0:T(8,128)(2,1)}) %all-gather.4.cloned.1.call-update) | async-done | bytes 8388624 | tf_op jit(solution)/shard_map/all_gather | solution.py:57
  454.1 6.3 %convolution_bitcast_fusion.2 = f32[512,128]{1,0:T(8,128)S(1)} fusion(bf16[8,512,1024]{2,1,0:T(8,128)(2,1)} %all-gather.4.cloned.1.call-done, bf16[8,128,1024]{2,1,0:T(8,128)(2,1)} %all_to_all.20), kind=kOutput, calls=%fused_computation.9 | convolution fusion | flops 1073741824 | bytes 10747904 | tf_op jit(solution)/shard_map/rnk,rjk->nj/dot_general | solution.py:55
  460.5 1.0 fusion.1
  (30 shorter events, 0.3 us)
Async XLA Ops:
  7.2 71.5 %copy-start = (bf16[32,128,128]{2,1,0:T(8,128)(2,1)S(1)}, bf16[32,128,128]{2,1,0:T(8,128)(2,1)}, u32[]{:S(2)}) copy-start(bf16[32,128,128]{2,1,0:T(8,128)(2,1)} %param.16) | copy-start | bytes 3145732
  7.2 78.6 %all-gather.8.cloned.1.call-start = ((), (), s32[]{:S(2)}) async-start(), calls=%async_computation.4 | async-start | bytes 1179648 | tf_op jit(solution)/shard_map/all_gather | solution.py:64
  12.3 15.0 %copy-start.3 = (bf16[8,16,128]{2,1,0:T(8,128)(2,1)S(1)}, bf16[8,16,128]{2,1,0:T(8,128)(2,1)}, u32[]{:S(2)}) copy-start(bf16[8,16,128]{2,1,0:T(8,128)(2,1)} %param.15) | copy-start | bytes 98308
  12.3 16.5 %copy-start.6 = (s32[32]{0:T(128)S(1)}, s32[32]{0:T(128)}, u32[]{:S(2)}) copy-start(s32[32]{0:T(128)} %param.19) | copy-start | bytes 388
  12.3 16.5 %copy-start.7 = (s32[32]{0:T(128)S(1)}, s32[32]{0:T(128)}, u32[]{:S(2)}) copy-start(s32[32]{0:T(128)} %param.18) | copy-start | bytes 388
  12.3 16.5 %copy-start.8 = (s32[32]{0:T(128)S(1)}, s32[32]{0:T(128)}, u32[]{:S(2)}) copy-start(s32[32]{0:T(128)} %param.17) | copy-start | bytes 388
  12.3 64.7 %all-to-all-start = ((bf16[64,128,128]{2,1,0:T(8,128)(2,1)}), bf16[64,128,128]{2,1,0:T(8,128)(2,1)S(1)}, u32[]{:S(2)}, u32[]{:S(2)}) async-start(bf16[64,128,128]{2,1,0:T(8,128)(2,1)} %copy.38), calls=%async_computation | async-start | bytes 4194304 | tf_op jit(solution)/shard_map/all_to_all | solution.py:37
  27.3 117.5 %all-gather.6.cloned.1.call-start = ((), (), s32[]{:S(2)}) async-start(), calls=%async_computation.3 | async-start | bytes 2129920 | tf_op jit(solution)/shard_map/all_gather | solution.py:53
  28.0 323.8 %all-reduce.2.cloned.1.call-start = ((), (), s32[]{:S(2)}) async-start(), calls=%async_computation.5 | async-start | bytes 8388608 | tf_op jit(solution)/shard_map/psum | solution.py:69
  85.7 4.9 %copy-start.1 = (bf16[32,128,128]{2,1,0:T(8,128)(2,1)}, bf16[32,128,128]{2,1,0:T(8,128)(2,1)S(1)}, u32[]{:S(2)}) copy-start(bf16[32,128,128]{2,1,0:T(8,128)(2,1)S(1)} %copy.41) | copy-start | bytes 3145732
  90.6 363.5 %all-gather.4.cloned.1.call-start = ((), (), s32[]{:S(2)}) async-start(), calls=%async_computation.2 | async-start | bytes 9437184 | tf_op jit(solution)/shard_map/all_gather | solution.py:57
  144.7 212.2 %all-to-all-start.1 = ((bf16[8,1024,128]{2,0,1:T(8,128)(2,1)}), bf16[8,1024,128]{2,0,1:T(8,128)(2,1)}, u32[]{:S(2)}, u32[]{:S(2)}) async-start(bf16[8,1024,128]{2,0,1:T(8,128)(2,1)} %all-gather.6.cloned.1.call-done), calls=%async_computation.1 | async-start | bytes 4194304 | tf_op jit(solution)/shard_map/all_to_all | solution.py:54
  362.3 98.1 %copy-start.2 = (bf16[512,128]{1,0:T(8,128)(2,1)S(1)}, bf16[512,128]{1,0:T(8,128)(2,1)}, u32[]{:S(2)}) copy-start(bf16[512,128]{1,0:T(8,128)(2,1)} %param.12) | copy-start | bytes 393220
  362.3 98.1 %copy-start.4 = (f32[3,128]{1,0:T(4,128)S(1)}, f32[3,128]{1,0:T(4,128)}, u32[]{:S(2)}) copy-start(f32[3,128]{1,0:T(4,128)} %param.14) | copy-start | bytes 4612
  362.3 98.1 %copy-start.5 = (s32[512]{0:T(512)S(1)}, s32[512]{0:T(512)}, u32[]{:S(2)}) copy-start(s32[512]{0:T(512)} %param.13) | copy-start | bytes 6148
Sparse Core Ops, SparseCore 0:
  10.0 44.3 all-gather.7
  58.3 86.3 all-gather.5
  148.3 203.4 all-reduce.1
  353.9 100.2 all-gather.3
where the time goes:
time: 471 us; the launch traced here: 468 us
  waiting for transfers between devices  395 us (84%)
  starting transfers between devices  21.6 us (5%)
  matrix products  18.1 us (4%)
  local copies, waits for them, and re-layouts  15.5 us (3%)
  between operations  14.6 us (3%)
    psum x1, waiting for transfers between devices, body(): summed = lax.psum(weight_terms, 'dom')  201 us
    all_gather x1, waiting for transfers between devices, body(): lax.all_gather(block_grad, 'col', axis=2, tiled=True)  91.8 us
    all_gather x1, waiting for transfers between devices, body(): weight_full = lax.all_gather(weights, 'dom', axis=1, tiled=True)  53.5 us
    all_to_all x1, waiting for transfers between devices, body(): lax.all_to_all(outgoing, 'dom', split_axis=0, concat_axis=0, tiled=True)  48.1 us
    all_to_all x1, starting transfers between devices, body(): lax.all_to_all(outgoing, 'dom', split_axis=0, concat_axis=0, tiled=True)  15 us
  transfers between devices with their start and end apart: 6, of which 4 were waited for; matrix products, arithmetic and copies ran while one was open for 6% of the time, Pallas kernels for 0%

commit v1 on v0

v1 whole, which is shorter than its diff:
```python
import math

import jax
import jax.numpy as jnp
from jax import lax
from jax.experimental import pallas as pl
from jax.experimental.pallas import tpu as pltpu
from jax.sharding import Mesh, PartitionSpec as P

BF = jnp.bfloat16
F32 = jnp.float32
DOM = ("z", "x", "core")


def cost(flops, nbytes):
    return pl.CostEstimate(flops=flops, bytes_accessed=nbytes, transcendentals=0)


def whole():
    return pl.BlockSpec(memory_space=pltpu.VMEM)


def pick_blocks(wanted, blocks):
    count = wanted.shape[0]
    _, rows, cols = blocks.shape
    group = 16

    def kernel(want_ref, blk_ref, out_ref):
        base = pl.program_id(0) * group
        for i in range(group):
            out_ref[i] = blk_ref[jnp.maximum(want_ref[base + i], 0)]

    return pl.pallas_call(
        kernel,
        out_shape=jax.ShapeDtypeStruct((count, rows, cols), blocks.dtype),
        grid_spec=pltpu.PrefetchScalarGridSpec(
            num_scalar_prefetch=1,
            grid=(count // group,),
            in_specs=[pl.BlockSpec(blocks.shape, lambda i, w: (0, 0, 0))],
            out_specs=pl.BlockSpec((group, rows, cols), lambda i, w: (i, 0, 0)),
        ),
        cost_estimate=cost(0, count * rows * cols * 2),
        name="pick_blocks",
    )(wanted, blocks)


def merge_tiles(peer, slot, count, tiles, incoming, relations, block_count):
    slots, size, _ = tiles.shape
    cols = incoming.shape[2]
    half = relations // 2
    buckets = relations * block_count

    def kernel(peer_ref, slot_ref, count_ref, tile_ref, inc_ref, out_ref, con, acc):
        acc[...] = jnp.zeros_like(acc)
        for t in range(slots):
            con[t] = lax.dot_general(
                tile_ref[t],
                inc_ref[peer_ref[t]],
                (((0,), (0,)), ((), ())),
                preferred_element_type=F32,
            )
        for t in range(slots):
            where = jnp.where(t < count_ref[0], slot_ref[t], buckets)
            acc[where] += con[t]
        for r in range(relations):
            for b in range(block_count):
                out_ref[r // half, b * size : (b + 1) * size, (r % half) * cols : (r % half + 1) * cols] = acc[
                    r * block_count + b
                ].astype(BF)

    smem = pl.BlockSpec(memory_space=pltpu.SMEM)
    return pl.pallas_call(
        kernel,
        out_shape=jax.ShapeDtypeStruct((2, block_count * size, half * cols), BF),
        in_specs=[smem, smem, smem, whole(), whole()],
        out_specs=whole(),
        scratch_shapes=[
            pltpu.VMEM((slots, size, cols), F32),
            pltpu.VMEM((buckets + 1, size, cols), F32),
        ],
        compiler_params=pltpu.CompilerParams(vmem_limit_bytes=24 << 20),
        cost_estimate=cost(2 * slots * size * size * cols, 4 << 20),
        name="merge_tiles",
    )(peer, slot, count, tiles, incoming)


def flip(pieces):
    n = len(pieces)
    rows, cols = pieces[0].shape

    def kernel(*refs):
        out_ref = refs[n]
        for i in range(n):
            out_ref[i] = refs[i][...].T

    return pl.pallas_call(
        kernel,
        out_shape=jax.ShapeDtypeStruct((n, cols, rows), pieces[0].dtype),
        in_specs=[whole()] * n,
        out_specs=whole(),
        cost_estimate=cost(0, 2 * n * rows * cols * 2),
        name="flip",
    )(*pieces)


def fold(parts, scale, copies):
    n, rows, cols = parts.shape
    steps = 4 if rows > 512 else 1
    block = rows // steps

    def kernel(in_ref, out_ref):
        total = in_ref[0].astype(F32)
        for i in range(1, n):
            total = total + in_ref[i].astype(F32)
        if scale is not None:
            total = total * scale
        total = total.astype(BF)
        for i in range(copies):
            out_ref[i] = total

    return pl.pallas_call(
        kernel,
        out_shape=jax.ShapeDtypeStruct((copies, rows, cols), BF),
        grid=(steps,),
        in_specs=[pl.BlockSpec((n, block, cols), lambda i: (0, i, 0))],
        out_specs=pl.BlockSpec((copies, block, cols), lambda i: (0, i, 0)),
        cost_estimate=cost(n * rows * cols, (n + copies) * rows * cols * 2),
        name="fold",
    )(parts)


def weight_terms(which, feature_t, block_grad, relations):
    n, jw, rows = feature_t.shape
    wide = block_grad.shape[2]
    half = relations // 2
    cols = wide // half

    def kernel(which_ref, f_ref, g_ref, out_ref):
        d = jnp.dot(f_ref[0], g_ref[0], preferred_element_type=F32)
        for r in range(half):
            out_ref[r] = d[:, r * cols : (r + 1) * cols]

    return pl.pallas_call(
        kernel,
        out_shape=jax.ShapeDtypeStruct((half, n * jw, cols), F32),
        grid_spec=pltpu.PrefetchScalarGridSpec(
            num_scalar_prefetch=1,
            grid=(n,),
            in_specs=[
                pl.BlockSpec((1, jw, rows), lambda c, w: (c, 0, 0)),
                pl.BlockSpec((1, rows, wide), lambda c, w: (w[0], 0, 0)),
            ],
            out_specs=pl.BlockSpec((half, jw, cols), lambda c, w: (0, lax.rem(w[1] - c + n, n), 0)),
        ),
        cost_estimate=cost(2 * n * jw * rows * wide, 4 << 20),
        name="weight_terms",
    )(which, feature_t, block_grad)


def feature_terms(block_grad, weight_rows, n):
    _, rows, wide = block_grad.shape
    jw = weight_rows.shape[0] // n

    def kernel(g_ref, w_ref, out_ref):
        total = None
        for h in range(2):
            part = lax.dot_general(
                g_ref[h],
                w_ref[:, h * wide : (h + 1) * wide],
                (((1,), (1,)), ((), ())),
                preferred_element_type=F32,
            )
            total = part if total is None else total + part
        out_ref[0] = total

    return pl.pallas_call(
        kernel,
        out_shape=jax.ShapeDtypeStruct((n, rows, jw), F32),
        grid=(n,),
        in_specs=[
            pl.BlockSpec(block_grad.shape, lambda c: (0, 0, 0)),
            pl.BlockSpec((jw, 2 * wide), lambda c: (c, 0)),
        ],
        out_specs=pl.BlockSpec((1, rows, jw), lambda c: (c, 0, 0)),
        cost_estimate=cost(4 * n * jw * rows * wide, 4 << 20),
        name="feature_terms",
    )(block_grad, weight_rows)


def exchange(parts, axis):
    return lax.all_to_all(parts, axis, split_axis=0, concat_axis=0, tiled=True)


def repeat(part, n):
    return jnp.broadcast_to(part[None], (n,) + part.shape)


def body(
    feature,
    cotangent,
    node_type,
    self_gain,
    weights,
    tile_values,
    tile_rel,
    tile_src,
    tile_peer,
    tile_count,
    send_block,
):
    partitions = lax.axis_size(DOM)
    row_count, col_width = cotangent.shape
    tile_size = tile_values.shape[1]
    block_count = row_count // tile_size
    relations, w_rows, _ = weights.shape
    half = relations // 2
    columns = lax.axis_size("y")
    nx = lax.axis_size("x")
    nz = lax.axis_size("z")
    core = lax.axis_index("core").astype(jnp.int32)

    outgoing = pick_blocks(send_block[0], cotangent.reshape(block_count, tile_size, col_width))
    incoming = exchange(outgoing, DOM)
    column = lax.axis_index("y").astype(jnp.int32)
    weight_rows = lax.all_gather(
        weights.transpose(1, 0, 2).reshape(w_rows, relations * col_width), DOM, axis=0, tiled=True
    )
    pieces = [feature] + [
        lax.ppermute(feature, "y", [(i, (i + k) % columns) for i in range(columns)]) for k in range(1, columns)
    ]
    feature_t = flip(pieces)
    block_grad = merge_tiles(
        tile_peer,
        tile_rel * block_count + tile_src,
        tile_count,
        tile_values,
        incoming,
        relations,
        block_count,
    )

    give = weight_terms(jnp.stack([1 - core, column]), feature_t, block_grad, relations)
    got = lax.ppermute(give, "core", [(0, 1), (1, 0)])
    keep = weight_terms(jnp.stack([core, column]), feature_t, block_grad, relations)
    j_count = keep.shape[1]
    mine = (keep + got).astype(BF).reshape(nx, half * j_count // nx, col_width)
    mine = fold(exchange(mine, "x"), None, 1)
    mine, late_grad, late_rows = lax.optimization_barrier((mine, block_grad, weight_rows))
    norm_scale = 1.0 / math.sqrt(row_count * partitions)
    mine = fold(exchange(mine.reshape(nz, -1, col_width), "z"), norm_scale, nz)
    mine = exchange(mine, "z").reshape(-1, col_width)
    mine = exchange(repeat(mine, nx), "x").reshape(-1, col_width)
    weight_grad = exchange(repeat(mine, 2), "core").reshape(relations, j_count, col_width)

    partial = feature_terms(late_grad, late_rows, columns)
    partial = lax.psum_scatter(partial, "y", scatter_dimension=0, tiled=True)[0]
    kind = node_type[:, None]
    gains = jnp.where(kind == 0, self_gain[0:1], jnp.where(kind == 1, self_gain[1:2], self_gain[2:3]))
    self_term = cotangent.astype(F32) * gains
    feature_grad = (partial + self_term).astype(BF)
    return (feature_grad, weight_grad)


def solution(mesh):
    fine = Mesh(mesh.devices.reshape(8, 4, 2, 8), ("z", "x", "core", "y"))
    return jax.shard_map(
        body,
        mesh=fine,
        in_specs=(
            P(DOM, "y"),
            P(DOM, "y"),
            P(DOM),
            P(None, "y"),
            P(None, DOM, "y"),
            P(DOM, None, None),
            P(DOM),
            P(DOM),
            P(DOM),
            P(DOM),
            P(DOM, None),
        ),
        out_specs=(P(DOM, "y"), P(None, None, "y")),
        check_vma=False,
    )
```

time: 471 us -> 195 us (0.41)
  waiting for transfers between devices: 395 us -> 28.1 us
  blocking collectives: 0 us -> 55 us
  Pallas kernels: 0 us -> 34.2 us
  starting transfers between devices: 21.6 us -> 51 us
  matrix products: 18.1 us -> 0 us
  local copies, waits for them, and re-layouts: 15.5 us -> 5.81 us
    psum x1 -> x0, waiting for transfers between devices: 201 us -> none  [body(): summed = lax.psum(weight_terms, 'dom')]
    all_gather x3 -> x1, waiting for transfers between devices: 145 us -> 0.01 us  [body(): lax.all_gather(weights.transpose(1, 0, 2).reshape(w_rows, relations * col...]
    all_to_all x0 -> x4, blocking collectives: none -> 55 us  [exchange(): return lax.all_to_all(parts, axis, split_axis=0, concat_axis=0, tiled=True)]
    pallas_call x0 -> x8, Pallas kernels: none -> 34.2 us  [the longest x2 14.3 us: weight_terms(): pl.pallas_call(kernel, out_shape=jax.ShapeDtypeStruct((half, n * jw, cols...]
    ppermute x0 -> x8, starting transfers between devices: none -> 32.5 us  [the longest x7 28.4 us: body(): lax.ppermute(feature, 'y', [(i, (i + k) % columns) for i in range(columns)])]
    all_to_all x2, waiting for transfers between devices: 48.1 us -> 17.8 us  [exchange(): return lax.all_to_all(parts, axis, split_axis=0, concat_axis=0, tiled=True)]
    dot_general x6 -> x0, matrix products: 18.1 us -> none  [the longest x1 6.31 us: body(): jnp.einsum('rnk,rjk->nj', lax.all_gather(block_grad, 'col', axis=2, tiled...]
    ppermute x0 -> x8, waiting for transfers between devices: none -> 10.2 us  [the longest x7 10.2 us: body(): lax.ppermute(feature, 'y', [(i, (i + k) % columns) for i in range(columns)])]
  transfers between devices with their start and end apart: 6 -> 12, of which waited for: 4 -> 5; matrix products, arithmetic and copies ran while one was open for 6% -> 3% of each run, Pallas kernels for 0% -> 12%
where the time goes in v1:
time: 195 us; the launch traced here: 194 us
  blocking collectives  55 us (28%)
  starting transfers between devices  51 us (26%)
  Pallas kernels  34.2 us (18%)
  waiting for transfers between devices  28.1 us (14%)
  between operations  14.9 us (8%)
  local copies, waits for them, and re-layouts  5.81 us (3%)
  other arithmetic  4.84 us (2%)
    all_to_all x4, blocking collectives, exchange(): return lax.all_to_all(parts, axis, split_axis=0, concat_axis=0, tiled=True)  55 us
    ppermute x7, starting transfers between devices, body(): lax.ppermute(feature, 'y', [(i, (i + k) % columns) for i in range(columns)])  28.4 us
    all_to_all x2, starting transfers between devices, exchange(): return lax.all_to_all(parts, axis, split_axis=0, concat_axis=0, tiled=True)  18.5 us
    all_to_all x2, waiting for transfers between devices, exchange(): return lax.all_to_all(parts, axis, split_axis=0, concat_axis=0, tiled=True)  17.8 us
    pallas_call x2, Pallas kernels, weight_terms(): pl.pallas_call(kernel, out_shape=jax.ShapeDtypeStruct((half, n * jw, cols...  14.3 us
    ppermute x7, waiting for transfers between devices, body(): lax.ppermute(feature, 'y', [(i, (i + k) % columns) for i in range(columns)])  10.2 us
    pallas_call x1, Pallas kernels, feature_terms(): pl.pallas_call(kernel, out_shape=jax.ShapeDtypeStruct((n, rows, jw), F32)...  7.58 us
    pallas_call x2, Pallas kernels, fold(): pl.pallas_call(kernel, out_shape=jax.ShapeDtypeStruct((copies, rows, cols...  4.94 us
  transfers between devices with their start and end apart: 12, of which 5 were waited for; matrix products, arithmetic and copies ran while one was open for 3% of the time, Pallas kernels for 12%

profile of v1, /device:TPU:1, one launch (start us, length us, event | category | flops | bytes accessed | tf_op | source)
XLA Modules:
  0.0 194.0 jit_solution(10239800545615994817)
XLA Ops:
  7.2 3.5 %pick_blocks.1 = bf16[64,128,128]{2,1,0:T(8,128)(2,1)} custom-call(s32[64]{0:T(128)} %bitcast.30, bf16[4,128,128]{2,1,0:T(8,128)(2,1)} %bitcast.29), custom_call_target="tpu_custom_call" | custom-call | bytes 2097152 | tf_op jit(solution)/shard_map/pick_blocks/pallas_call | solution.py:33
  10.7 15.0 %all-to-all-start = ((bf16[64,128,128]{2,1,0:T(8,128)(2,1)}), bf16[64,128,128]{2,1,0:T(8,128)(2,1)S(1)}, u32[]{:S(2)}, u32[]{:S(2)}) async-start(bf16[64,128,128]{2,1,0:T(8,128)(2,1)} %pick_blocks.1), calls=%async_computation | async-start | bytes 4194304 | tf_op jit(solution)/shard_map/all_to_all | solution.py:191
  26.5 3.2 %collective-permute-start = (bf16[512,128]{1,0:T(8,128)(2,1)S(1)}, bf16[512,128]{1,0:T(8,128)(2,1)S(1)}, u32[]{:S(2)}, u32[]{:S(2)}) collective-permute-start(bf16[512,128]{1,0:T(8,128)(2,1)S(1)} %copy-done.6), channel_id=1, source_target_pairs={{0,1},{1,2},{2,3},{3,4},{4,5},{5,6},{6,7},{7,0},{8,9},{9,10},{10,1... | collective-permute-start | bytes 393224 | tf_op jit(solution)/shard_map/ppermute | solution.py:229
  29.7 4.2 %collective-permute-start.1 = (bf16[512,128]{1,0:T(8,128)(2,1)S(1)}, bf16[512,128]{1,0:T(8,128)(2,1)S(1)}, u32[]{:S(2)}, u32[]{:S(2)}) collective-permute-start(bf16[512,128]{1,0:T(8,128)(2,1)S(1)} %copy-done.6), channel_id=1, source_target_pairs={{0,2},{1,3},{2,4},{3,5},{4,6},{5,7},{6,0},{7,1},{8,10},{9,11},{10,... | collective-permute-start | bytes 393224 | tf_op jit(solution)/shard_map/ppermute | solution.py:229
  34.0 4.6 %collective-permute-start.2 = (bf16[512,128]{1,0:T(8,128)(2,1)S(1)}, bf16[512,128]{1,0:T(8,128)(2,1)}, u32[]{:S(2)}, u32[]{:S(2)}) collective-permute-start(bf16[512,128]{1,0:T(8,128)(2,1)S(1)} %copy-done.6), channel_id=1, source_target_pairs={{0,3},{1,4},{2,5},{3,6},{4,7},{5,0},{6,1},{7,2},{8,11},{9,12},{10,... | collective-permute-start | bytes 393224 | tf_op jit(solution)/shard_map/ppermute | solution.py:229
  38.6 3.5 %collective-permute-start.3 = (bf16[512,128]{1,0:T(8,128)(2,1)S(1)}, bf16[512,128]{1,0:T(8,128)(2,1)}, u32[]{:S(2)}, u32[]{:S(2)}) collective-permute-start(bf16[512,128]{1,0:T(8,128)(2,1)S(1)} %copy-done.6), channel_id=1, source_target_pairs={{0,4},{1,5},{2,6},{3,7},{4,0},{5,1},{6,2},{7,3},{8,12},{9,13},{10,... | collective-permute-start | bytes 393224 | tf_op jit(solution)/shard_map/ppermute | solution.py:229
  42.2 4.9 %collective-permute-start.4 = (bf16[512,128]{1,0:T(8,128)(2,1)S(1)}, bf16[512,128]{1,0:T(8,128)(2,1)}, u32[]{:S(2)}, u32[]{:S(2)}) collective-permute-start(bf16[512,128]{1,0:T(8,128)(2,1)S(1)} %copy-done.6), channel_id=1, source_target_pairs={{0,5},{1,6},{2,7},{3,0},{4,1},{5,2},{6,3},{7,4},{8,13},{9,14},{10,... | collective-permute-start | bytes 393224 | tf_op jit(solution)/shard_map/ppermute | solution.py:229
  47.1 5.0 %collective-permute-start.5 = (bf16[512,128]{1,0:T(8,128)(2,1)S(1)}, bf16[512,128]{1,0:T(8,128)(2,1)}, u32[]{:S(2)}, u32[]{:S(2)}) collective-permute-start(bf16[512,128]{1,0:T(8,128)(2,1)S(1)} %copy-done.6), channel_id=1, source_target_pairs={{0,6},{1,7},{2,0},{3,1},{4,2},{5,3},{6,4},{7,5},{8,14},{9,15},{10,... | collective-permute-start | bytes 393224 | tf_op jit(solution)/shard_map/ppermute | solution.py:229
  52.7 3.0 %collective-permute-start.6 = (bf16[512,128]{1,0:T(8,128)(2,1)S(1)}, bf16[512,128]{1,0:T(8,128)(2,1)}, u32[]{:S(2)}, u32[]{:S(2)}) collective-permute-start(bf16[512,128]{1,0:T(8,128)(2,1)S(1)} %copy-done.6), channel_id=1, source_target_pairs={{0,7},{1,0},{2,1},{3,2},{4,3},{5,4},{6,5},{7,6},{8,15},{9,8},{10,9... | collective-permute-start | bytes 393224 | tf_op jit(solution)/shard_map/ppermute | solution.py:229
  57.0 2.8 %collective-permute-done.4.refs_5_ = bf16[512,128]{1,0:T(8,128)(2,1)} collective-permute-done((bf16[512,128]{1,0:T(8,128)(2,1)S(1)}, bf16[512,128]{1,0:T(8,128)(2,1)}, u32[]{:S(2)}, u32[]{:S(2)}) %collective-permute-start.4) | collective-permute-done | bytes 131104 | tf_op jit(solution)/shard_map/ppermute | solution.py:229
  59.8 6.3 %collective-permute-done.5.refs_6_ = bf16[512,128]{1,0:T(8,128)(2,1)} collective-permute-done((bf16[512,128]{1,0:T(8,128)(2,1)S(1)}, bf16[512,128]{1,0:T(8,128)(2,1)}, u32[]{:S(2)}, u32[]{:S(2)}) %collective-permute-start.5) | collective-permute-done | bytes 131104 | tf_op jit(solution)/shard_map/ppermute | solution.py:229
  67.2 2.6 %flip.1.f_ref = bf16[8,128,512]{2,1,0:T(8,128)(2,1)} custom-call(bf16[512,128]{1,0:T(8,128)(2,1)} %refs_0_.1, bf16[512,128]{1,0:T(8,128)(2,1)} %copy-done.7, bf16[512,128]{1,0:T(8,128)(2,1)} %copy-done.8, bf16[512,128]{1,0:T(8,128)(2,1)} %collective-permute-done.2.refs_3_, bf16[512,128]{1,0:T(8,128)(2,1)} %collective-permute-done.3.refs_4_, ...), custom_call_target="tpu_custom_call" | custom-call | bytes 2097152 | tf_op jit(solution)/shard_map/flip/pallas_call | solution.py:96
  69.8 6.8 %all-to-all-done.inc_ref = bf16[64,128,128]{2,1,0:T(8,128)(2,1)S(1)} async-done(((bf16[64,128,128]{2,1,0:T(8,128)(2,1)}), bf16[64,128,128]{2,1,0:T(8,128)(2,1)S(1)}, u32[]{:S(2)}, u32[]{:S(2)}) %all-to-all-start) | async-done | bytes 2097184 | tf_op jit(solution)/shard_map/all_to_all | solution.py:191
  78.9 7.1 %weight_terms.3 = f32[4,1024,128]{2,1,0:T(8,128)} custom-call(s32[2]{0:T(128)} %pad_add_fusion.1.which_ref, bf16[8,128,512]{2,1,0:T(8,128)(2,1)} %flip.1.f_ref, bf16[2,512,512]{2,1,0:T(8,128)(2,1)} %copy-done.1), custom_call_target="tpu_custom_call" | custom-call | flops 536870912 | bytes 4194304 | tf_op jit(solution)/shard_map/weight_terms/pallas_call | solution.py:143
  86.1 4.0 %collective-permute-start.7 = (f32[4,1024,128]{2,1,0:T(8,128)}, f32[4,1024,128]{2,1,0:T(8,128)S(1)}, u32[]{:S(2)}, u32[]{:S(2)}) collective-permute-start(f32[4,1024,128]{2,1,0:T(8,128)} %weight_terms.3), channel_id=1, source_target_pairs={{0,8},{8,0},{1,9},{9,1},{2,10},{10,2},{3,11},{11,3},{4,12},{12,4},... | collective-permute-start | bytes 6291464 | tf_op jit(solution)/shard_map/ppermute | solution.py:243
  90.7 7.1 %weight_terms.2 = f32[4,1024,128]{2,1,0:T(8,128)} custom-call(s32[2]{0:T(128)} %pad_add_fusion.which_ref, bf16[8,128,512]{2,1,0:T(8,128)(2,1)} %flip.1.f_ref, bf16[2,512,512]{2,1,0:T(8,128)(2,1)} %copy-done.1), custom_call_target="tpu_custom_call" | custom-call | flops 536870912 | bytes 4194304 | tf_op jit(solution)/shard_map/weight_terms/pallas_call | solution.py:143
  99.7 18.8 %all_to_all.30.in_ref = bf16[4,1024,128]{2,1,0:T(8,128)(2,1)} all-to-all(bf16[4,1024,128]{2,1,0:T(8,128)(2,1)S(1)} %add_convert_fusion), channel_id=1, replica_groups=mesh['z'=8,'x'=4,'core'=2,'y'=8] {'x'}, dimensions={0} | all-to-all | bytes 2097152 | tf_op jit(solution)/shard_map/all_to_all | solution.py:191
  118.5 3.2 %fold.2 = bf16[1,1024,128]{2,1,0:T(8,128)(2,1)} custom-call(bf16[4,1024,128]{2,1,0:T(8,128)(2,1)} %all_to_all.30.in_ref), custom_call_target="tpu_custom_call" | custom-call | flops 524288 | bytes 1310720 | tf_op jit(solution)/shard_map/fold/pallas_call | solution.py:121
  121.7 7.6 %feature_terms.1 = f32[8,512,128]{2,1,0:T(8,128)} custom-call(bf16[2,512,512]{2,1,0:T(8,128)(2,1)} %copy-done.1, bf16[1024,1024]{1,0:T(8,128)(2,1)} %all-gather.2.cloned.1.call-done.w_ref), custom_call_target="tpu_custom_call" | custom-call | flops 1073741824 | bytes 4194304 | tf_op jit(solution)/shard_map/feature_terms/pallas_call | solution.py:176
  130.3 13.2 %all_to_all.31.in_ref = bf16[8,128,128]{2,1,0:T(8,128)(2,1)} all-to-all(bf16[8,128,128]{2,1,0:T(8,128)(2,1)S(1)} %bitcast.27), channel_id=1, replica_groups=mesh['z'=8,'x'=4,'core'=2,'y'=8] {'z'}, dimensions={0} | all-to-all | bytes 524288 | tf_op jit(solution)/shard_map/all_to_all | solution.py:191
  145.2 12.8 %all_to_all.32 = bf16[8,128,128]{2,1,0:T(8,128)(2,1)S(1)} all-to-all(bf16[8,128,128]{2,1,0:T(8,128)(2,1)} %fold.3), channel_id=1, replica_groups=mesh['z'=8,'x'=4,'core'=2,'y'=8] {'z'}, dimensions={0} | all-to-all | bytes 524288 | tf_op jit(solution)/shard_map/all_to_all | solution.py:191
  159.1 3.5 %all-to-all-start.4 = ((bf16[4,1024,128]{2,1,0:T(8,128)(2,1)}), bf16[4,1024,128]{2,1,0:T(8,128)(2,1)S(1)}, u32[]{:S(2)}, u32[]{:S(2)}) async-start(bf16[4,1024,128]{2,1,0:T(8,128)(2,1)} %broadcast_in_dim.70), calls=%async_computation.5 | async-start | bytes 2097152 | tf_op jit(solution)/shard_map/all_to_all | solution.py:191
  162.7 11.0 %all-to-all-done.4 = bf16[4,1024,128]{2,1,0:T(8,128)(2,1)S(1)} async-done(((bf16[4,1024,128]{2,1,0:T(8,128)(2,1)}), bf16[4,1024,128]{2,1,0:T(8,128)(2,1)S(1)}, u32[]{:S(2)}, u32[]{:S(2)}) %all-to-all-start.4) | async-done | bytes 1048608 | tf_op jit(solution)/shard_map/all_to_all | solution.py:191
  173.8 10.2 %all_to_all.33 = bf16[2,4096,128]{2,1,0:T(8,128)(2,1)S(1)} all-to-all(bf16[2,4096,128]{2,1,0:T(8,128)(2,1)S(1)} %broadcast_in_dim.72), channel_id=1, replica_groups=mesh['z'=8,'x'=4,'core'=2,'y'=8] {'core'}, dimensions={0} | all-to-all | bytes 4194304 | tf_op jit(solution)/shard_map/all_to_all | solution.py:191
  (51 shorter events, 15.0 us)
Async XLA Ops:
  7.2 18.6 %copy-start = (bf16[8,16,128]{2,1,0:T(8,128)(2,1)S(1)}, bf16[8,16,128]{2,1,0:T(8,128)(2,1)}, u32[]{:S(2)}) copy-start(bf16[8,16,128]{2,1,0:T(8,128)(2,1)} %param.15) | copy-start | bytes 98308
  10.7 15.8 %copy-start.6 = (bf16[512,128]{1,0:T(8,128)(2,1)S(1)}, bf16[512,128]{1,0:T(8,128)(2,1)}, u32[]{:S(2)}) copy-start(bf16[512,128]{1,0:T(8,128)(2,1)} %refs_0_.1) | copy-start | bytes 393220
  10.7 44.9 %copy-start.11 = (s32[32]{0:T(128)S(1)}, s32[32]{0:T(128)}, u32[]{:S(2)}) copy-start(s32[32]{0:T(128)} %param.18) | copy-start | bytes 388
  10.7 45.0 %copy-start.12 = (s32[32]{0:T(128)S(1)}, s32[32]{0:T(128)}, u32[]{:S(2)}) copy-start(s32[32]{0:T(128)} %param.17) | copy-start | bytes 388
  10.7 65.9 %all-to-all-start = ((bf16[64,128,128]{2,1,0:T(8,128)(2,1)}), bf16[64,128,128]{2,1,0:T(8,128)(2,1)S(1)}, u32[]{:S(2)}, u32[]{:S(2)}) async-start(bf16[64,128,128]{2,1,0:T(8,128)(2,1)} %pick_blocks.1), calls=%async_computation | async-start | bytes 4194304 | tf_op jit(solution)/shard_map/all_to_all | solution.py:191
  25.7 50.9 %copy-start.2 = (bf16[32,128,128]{2,1,0:T(8,128)(2,1)S(1)}, bf16[32,128,128]{2,1,0:T(8,128)(2,1)}, u32[]{:S(2)}) copy-start(bf16[32,128,128]{2,1,0:T(8,128)(2,1)} %tile_ref.1) | copy-start | bytes 3145732
  25.7 50.9 %copy-start.3 = (s32[32]{0:T(128)S(1)}, s32[32]{0:T(128)}, u32[]{:S(2)}) copy-start(s32[32]{0:T(128)} %peer_ref.1) | copy-start | bytes 388
  25.7 96.0 %all-gather.2.cloned.1.call-start = ((), (), s32[]{:S(2)}) async-start(), calls=%async_computation.7 | async-start | bytes 2129920 | tf_op jit(solution)/shard_map/all_gather | solution.py:225
  26.5 157.5 %reduce-scatter.2.cloned.1.call-start = ((), (), s32[]{:S(2)}) async-start(), calls=%async_computation.8 | async-start | bytes 2359296 | tf_op jit(solution)/shard_map/reduce_scatter | solution.py:256
  26.5 20.5 %collective-permute-start = (bf16[512,128]{1,0:T(8,128)(2,1)S(1)}, bf16[512,128]{1,0:T(8,128)(2,1)S(1)}, u32[]{:S(2)}, u32[]{:S(2)}) collective-permute-start(bf16[512,128]{1,0:T(8,128)(2,1)S(1)} %copy-done.6), channel_id=1, source_target_pairs={{0,1},{1,2},{2,3},{3,4},{4,5},{5,6},{6,7},{7,0},{8,9},{9,10},{10,1... | collective-permute-start | bytes 393224 | tf_op jit(solution)/shard_map/ppermute | solution.py:229
  29.7 22.3 %collective-permute-start.1 = (bf16[512,128]{1,0:T(8,128)(2,1)S(1)}, bf16[512,128]{1,0:T(8,128)(2,1)S(1)}, u32[]{:S(2)}, u32[]{:S(2)}) collective-permute-start(bf16[512,128]{1,0:T(8,128)(2,1)S(1)} %copy-done.6), channel_id=1, source_target_pairs={{0,2},{1,3},{2,4},{3,5},{4,6},{5,7},{6,0},{7,1},{8,10},{9,11},{10,... | collective-permute-start | bytes 393224 | tf_op jit(solution)/shard_map/ppermute | solution.py:229
  34.0 23.0 %collective-permute-start.2 = (bf16[512,128]{1,0:T(8,128)(2,1)S(1)}, bf16[512,128]{1,0:T(8,128)(2,1)}, u32[]{:S(2)}, u32[]{:S(2)}) collective-permute-start(bf16[512,128]{1,0:T(8,128)(2,1)S(1)} %copy-done.6), channel_id=1, source_target_pairs={{0,3},{1,4},{2,5},{3,6},{4,7},{5,0},{6,1},{7,2},{8,11},{9,12},{10,... | collective-permute-start | bytes 393224 | tf_op jit(solution)/shard_map/ppermute | solution.py:229
  38.6 18.3 %collective-permute-start.3 = (bf16[512,128]{1,0:T(8,128)(2,1)S(1)}, bf16[512,128]{1,0:T(8,128)(2,1)}, u32[]{:S(2)}, u32[]{:S(2)}) collective-permute-start(bf16[512,128]{1,0:T(8,128)(2,1)S(1)} %copy-done.6), channel_id=1, source_target_pairs={{0,4},{1,5},{2,6},{3,7},{4,0},{5,1},{6,2},{7,3},{8,12},{9,13},{10,... | collective-permute-start | bytes 393224 | tf_op jit(solution)/shard_map/ppermute | solution.py:229
  42.2 17.6 %collective-permute-start.4 = (bf16[512,128]{1,0:T(8,128)(2,1)S(1)}, bf16[512,128]{1,0:T(8,128)(2,1)}, u32[]{:S(2)}, u32[]{:S(2)}) collective-permute-start(bf16[512,128]{1,0:T(8,128)(2,1)S(1)} %copy-done.6), channel_id=1, source_target_pairs={{0,5},{1,6},{2,7},{3,0},{4,1},{5,2},{6,3},{7,4},{8,13},{9,14},{10,... | collective-permute-start | bytes 393224 | tf_op jit(solution)/shard_map/ppermute | solution.py:229
  47.1 20.1 %copy-start.7 = (bf16[512,128]{1,0:T(8,128)(2,1)}, bf16[512,128]{1,0:T(8,128)(2,1)S(1)}, u32[]{:S(2)}) copy-start(bf16[512,128]{1,0:T(8,128)(2,1)S(1)} %collective-permute-done.refs_1_) | copy-start | bytes 393220
  47.1 19.0 %collective-permute-start.5 = (bf16[512,128]{1,0:T(8,128)(2,1)S(1)}, bf16[512,128]{1,0:T(8,128)(2,1)}, u32[]{:S(2)}, u32[]{:S(2)}) collective-permute-start(bf16[512,128]{1,0:T(8,128)(2,1)S(1)} %copy-done.6), channel_id=1, source_target_pairs={{0,6},{1,7},{2,0},{3,1},{4,2},{5,3},{6,4},{7,5},{8,14},{9,15},{10,... | collective-permute-start | bytes 393224 | tf_op jit(solution)/shard_map/ppermute | solution.py:229
  52.7 14.5 %collective-permute-start.6 = (bf16[512,128]{1,0:T(8,128)(2,1)S(1)}, bf16[512,128]{1,0:T(8,128)(2,1)}, u32[]{:S(2)}, u32[]{:S(2)}) collective-permute-start(bf16[512,128]{1,0:T(8,128)(2,1)S(1)} %copy-done.6), channel_id=1, source_target_pairs={{0,7},{1,0},{2,1},{3,2},{4,3},{5,4},{6,5},{7,6},{8,15},{9,8},{10,9... | collective-permute-start | bytes 393224 | tf_op jit(solution)/shard_map/ppermute | solution.py:229
  77.9 1.0 copy-start.1
  86.1 11.8 %collective-permute-start.7 = (f32[4,1024,128]{2,1,0:T(8,128)}, f32[4,1024,128]{2,1,0:T(8,128)S(1)}, u32[]{:S(2)}, u32[]{:S(2)}) collective-permute-start(f32[4,1024,128]{2,1,0:T(8,128)} %weight_terms.3), channel_id=1, source_target_pairs={{0,8},{8,0},{1,9},{9,1},{2,10},{10,2},{3,11},{11,3},{4,12},{12,4},... | collective-permute-start | bytes 6291464 | tf_op jit(solution)/shard_map/ppermute | solution.py:243
  129.3 0.9 copy-start.4
  145.2 17.5 %copy-start.9 = (s32[512]{0:T(512)S(1)}, s32[512]{0:T(512)}, u32[]{:S(2)}) copy-start(s32[512]{0:T(512)} %param.13) | copy-start | bytes 6148
  145.2 17.5 %copy-start.10 = (f32[3,128]{1,0:T(4,128)S(1)}, f32[3,128]{1,0:T(4,128)}, u32[]{:S(2)}) copy-start(f32[3,128]{1,0:T(4,128)} %param.14) | copy-start | bytes 4612
  159.1 14.5 %all-to-all-start.4 = ((bf16[4,1024,128]{2,1,0:T(8,128)(2,1)}), bf16[4,1024,128]{2,1,0:T(8,128)(2,1)S(1)}, u32[]{:S(2)}, u32[]{:S(2)}) async-start(bf16[4,1024,128]{2,1,0:T(8,128)(2,1)} %broadcast_in_dim.70), calls=%async_computation.5 | async-start | bytes 2097152 | tf_op jit(solution)/shard_map/all_to_all | solution.py:191
  173.8 10.2 %copy-start.5 = (bf16[512,128]{1,0:T(8,128)(2,1)S(1)}, bf16[512,128]{1,0:T(8,128)(2,1)}, u32[]{:S(2)}) copy-start(bf16[512,128]{1,0:T(8,128)(2,1)} %param.12) | copy-start | bytes 393220
  (1 other events, 0.6 us)
Sparse Core Ops, SparseCore 0:
  29.9 87.0 all-gather.1
  129.5 35.9 reduce-scatter.1

commit v2 on v1

v2 whole, which is shorter than its diff:
```python
import math

import jax
import jax.numpy as jnp
from jax import lax
from jax.experimental import pallas as pl
from jax.experimental.pallas import tpu as pltpu
from jax.sharding import Mesh, PartitionSpec as P

BF = jnp.bfloat16
F32 = jnp.float32
DOM = ("z", "x", "core")


def cost(flops, nbytes):
    return pl.CostEstimate(flops=flops, bytes_accessed=nbytes, transcendentals=0)


def whole():
    return pl.BlockSpec(memory_space=pltpu.VMEM)


def pick_blocks(wanted, blocks):
    count = wanted.shape[0]
    _, rows, cols = blocks.shape

    def kernel(want_ref, blk_ref, out_ref):
        for i in range(count):
            out_ref[i] = blk_ref[jnp.maximum(want_ref[i], 0)]

    return pl.pallas_call(
        kernel,
        out_shape=jax.ShapeDtypeStruct((count, rows, cols), blocks.dtype),
        in_specs=[pl.BlockSpec(memory_space=pltpu.SMEM), whole()],
        out_specs=whole(),
        cost_estimate=cost(0, count * rows * cols * 2),
        name="pick_blocks",
    )(wanted, blocks)


def merge_tiles(core, peer, slot, count, tiles, incoming, relations, block_count):
    slots, size, _ = tiles.shape
    cols = incoming.shape[2]
    half = relations // 2
    buckets = relations * block_count

    def kernel(core_ref, peer_ref, slot_ref, count_ref, tile_ref, inc_ref, keep_ref, give_ref, con, acc):
        acc[...] = jnp.zeros_like(acc)
        for t in range(slots):
            con[t] = lax.dot_general(
                tile_ref[t],
                inc_ref[peer_ref[t]],
                (((0,), (0,)), ((), ())),
                preferred_element_type=F32,
            )
        for t in range(slots):
            where = jnp.where(t < count_ref[0], slot_ref[t], buckets)
            acc[where] += con[t]
        first = core_ref[0] * (half * block_count)
        for ref, base in ((keep_ref, first), (give_ref, half * block_count - first)):
            for r in range(half):
                for b in range(block_count):
                    ref[b * size : (b + 1) * size, r * cols : (r + 1) * cols] = acc[base + r * block_count + b].astype(
                        BF
                    )

    smem = pl.BlockSpec(memory_space=pltpu.SMEM)
    return pl.pallas_call(
        kernel,
        out_shape=(jax.ShapeDtypeStruct((block_count * size, half * cols), BF),) * 2,
        in_specs=[smem, smem, smem, smem, whole(), whole()],
        out_specs=(whole(), whole()),
        scratch_shapes=[
            pltpu.VMEM((slots, size, cols), F32),
            pltpu.VMEM((buckets + 1, size, cols), F32),
        ],
        compiler_params=pltpu.CompilerParams(vmem_limit_bytes=24 << 20),
        cost_estimate=cost(2 * slots * size * size * cols, 4 << 20),
        name="merge_tiles",
    )(core, peer, slot, count, tiles, incoming)


def flip(column, pieces):
    n = len(pieces)
    rows, cols = pieces[0].shape

    def kernel(*refs):
        col_ref, out_ref = refs[0], refs[n + 1]
        for k in range(n):
            at = lax.rem(col_ref[0] - k + n, n)
            out_ref[pl.ds(pl.multiple_of(at * cols, cols), cols), :] = refs[k + 1][...].T

    return pl.pallas_call(
        kernel,
        out_shape=jax.ShapeDtypeStruct((n * cols, rows), pieces[0].dtype),
        in_specs=[pl.BlockSpec(memory_space=pltpu.SMEM)] + [whole()] * n,
        out_specs=whole(),
        cost_estimate=cost(0, 2 * n * rows * cols * 2),
        name="flip",
    )(column, *pieces)


def fold(parts, scale, copies):
    n, rows, cols = parts.shape

    def kernel(in_ref, out_ref):
        total = in_ref[0].astype(F32)
        for i in range(1, n):
            total = total + in_ref[i].astype(F32)
        if scale is not None:
            total = total * scale
        total = total.astype(BF)
        for i in range(copies):
            out_ref[i] = total

    return pl.pallas_call(
        kernel,
        out_shape=jax.ShapeDtypeStruct((copies, rows, cols), BF),
        in_specs=[whole()],
        out_specs=whole(),
        cost_estimate=cost(n * rows * cols, (n + copies) * rows * cols * 2),
        name="fold",
    )(parts)


def weight_terms(own_t, other_t, own_grad, other_grad, half):
    features, rows = own_t.shape
    wide = own_grad.shape[1]
    cols = wide // half
    group = 2

    def kernel(fa_ref, fb_ref, ga_ref, gb_ref, out_ref):
        d = jnp.dot(fa_ref[...], ga_ref[...], preferred_element_type=F32)
        d = d + jnp.dot(fb_ref[...], gb_ref[...], preferred_element_type=F32)
        for r in range(group):
            out_ref[r] = d[:, r * cols : (r + 1) * cols].astype(BF)

    grad_spec = pl.BlockSpec((rows, group * cols), lambda i: (0, i))
    return pl.pallas_call(
        kernel,
        out_shape=jax.ShapeDtypeStruct((half, features, cols), BF),
        grid=(half // group,),
        in_specs=[whole(), whole(), grad_spec, grad_spec],
        out_specs=pl.BlockSpec((group, features, cols), lambda i: (i, 0, 0)),
        compiler_params=pltpu.CompilerParams(vmem_limit_bytes=24 << 20),
        cost_estimate=cost(4 * features * rows * wide, 4 << 20),
        name="weight_terms",
    )(own_t, other_t, own_grad, other_grad)


def feature_terms(core, keep, give, weight_rows, n):
    rows, wide = keep.shape
    jw = weight_rows.shape[0] // n
    group = 2

    def kernel(core_ref, keep_ref, give_ref, w_ref, out_ref):
        first = pl.multiple_of(core_ref[0] * wide, wide)
        dims = (((1,), (1,)), ((), ()))
        d = lax.dot_general(keep_ref[...], w_ref[:, pl.ds(first, wide)], dims, preferred_element_type=F32)
        d = d + lax.dot_general(give_ref[...], w_ref[:, pl.ds(wide - first, wide)], dims, preferred_element_type=F32)
        for c in range(group):
            out_ref[c] = d[:, c * jw : (c + 1) * jw]

    return pl.pallas_call(
        kernel,
        out_shape=jax.ShapeDtypeStruct((n, rows, jw), F32),
        grid=(n // group,),
        in_specs=[
            pl.BlockSpec(memory_space=pltpu.SMEM),
            whole(),
            whole(),
            pl.BlockSpec((group * jw, 2 * wide), lambda c: (c, 0)),
        ],
        out_specs=pl.BlockSpec((group, rows, jw), lambda c: (c, 0, 0)),
        compiler_params=pltpu.CompilerParams(vmem_limit_bytes=24 << 20),
        cost_estimate=cost(4 * n * jw * rows * wide, 4 << 20),
        name="feature_terms",
    )(core, keep, give, weight_rows)


def exchange(parts, axis):
    return lax.all_to_all(parts, axis, split_axis=0, concat_axis=0, tiled=True)


def repeat(part, n):
    return jnp.broadcast_to(part[None], (n,) + part.shape)


def body(
    feature,
    cotangent,
    node_type,
    self_gain,
    weights,
    tile_values,
    tile_rel,
    tile_src,
    tile_peer,
    tile_count,
    send_block,
):
    partitions = lax.axis_size(DOM)
    row_count, col_width = cotangent.shape
    tile_size = tile_values.shape[1]
    block_count = row_count // tile_size
    relations, w_rows, _ = weights.shape
    half = relations // 2
    columns = lax.axis_size("y")
    nx = lax.axis_size("x")
    nz = lax.axis_size("z")
    core = lax.axis_index("core").astype(jnp.int32)[None]
    column = lax.axis_index("y").astype(jnp.int32)[None]
    swap = [(0, 1), (1, 0)]

    w_shard = weights.transpose(1, 0, 2).reshape(w_rows, relations * col_width)
    w_shard, wanted = lax.optimization_barrier((w_shard, send_block[0]))
    weight_rows = lax.all_gather(w_shard, DOM, axis=0, tiled=True)
    outgoing = pick_blocks(wanted, cotangent.reshape(block_count, tile_size, col_width))
    incoming = exchange(outgoing, DOM)
    pieces = [feature] + [
        lax.ppermute(feature, "y", [(i, (i + k) % columns) for i in range(columns)]) for k in range(1, columns)
    ]
    own_t = flip(column, pieces)
    other_t = lax.ppermute(own_t, "core", swap)
    keep, give = merge_tiles(
        core,
        tile_peer,
        tile_rel * block_count + tile_src,
        tile_count,
        tile_values,
        incoming,
        relations,
        block_count,
    )

    mine = weight_terms(own_t, other_t, keep, lax.ppermute(give, "core", swap), half)
    j_count = mine.shape[1]
    mine = mine.reshape(nx, half * j_count // nx, col_width)
    mine = fold(exchange(mine, "x"), None, 1)
    mine, late_keep, late_give, late_rows = lax.optimization_barrier((mine, keep, give, weight_rows))
    norm_scale = 1.0 / math.sqrt(row_count * partitions)
    mine = fold(exchange(mine.reshape(nz, -1, col_width), "z"), norm_scale, nz)
    mine = exchange(mine, "z").reshape(-1, col_width)
    mine = exchange(repeat(mine, nx), "x").reshape(-1, col_width)
    weight_grad = exchange(repeat(mine, 2), "core").reshape(relations, j_count, col_width)

    partial = feature_terms(core, late_keep, late_give, late_rows, columns)
    partial = lax.psum_scatter(partial, "y", scatter_dimension=0, tiled=True)[0]
    kind = node_type[:, None]
    gains = jnp.where(kind == 0, self_gain[0:1], jnp.where(kind == 1, self_gain[1:2], self_gain[2:3]))
    self_term = cotangent.astype(F32) * gains
    feature_grad = (partial + self_term).astype(BF)
    return (feature_grad, weight_grad)


def solution(mesh):
    fine = Mesh(mesh.devices.reshape(8, 4, 2, 8), ("z", "x", "core", "y"))
    return jax.shard_map(
        body,
        mesh=fine,
        in_specs=(
            P(DOM, "y"),
            P(DOM, "y"),
            P(DOM),
            P(None, "y"),
            P(None, DOM, "y"),
            P(DOM, None, None),
            P(DOM),
            P(DOM),
            P(DOM),
            P(DOM),
            P(DOM, None),
        ),
        out_specs=(P(DOM, "y"), P(None, None, "y")),
        check_vma=False,
    )
```

time: 195 us -> 193 us (0.990)
  Pallas kernels: 34.2 us -> 15.8 us
  waiting for transfers between devices: 28.1 us -> 35.1 us
  blocking collectives: 55 us -> 59.7 us
  local copies, waits for them, and re-layouts: 5.81 us -> 10.2 us
  other arithmetic: 4.84 us -> 1.82 us
  starting transfers between devices: 51 us -> 53.9 us
    pallas_call x4 -> x3, Pallas kernels: 18.2 us -> 6.62 us  [the longest x1 2.72 us: weight_terms(): pl.pallas_call(kernel, out_shape=jax.ShapeDtypeStruct((half, features, co...]
    all_gather x1, waiting for transfers between devices: 0.01 us -> 6.14 us  [body(): weight_rows = lax.all_gather(w_shard, DOM, axis=0, tiled=True)]
    all_to_all x4, blocking collectives: 55 us -> 59.7 us  [exchange(): return lax.all_to_all(parts, axis, split_axis=0, concat_axis=0, tiled=True)]
    pallas_call x1, Pallas kernels: 7.58 us -> 3.03 us  [feature_terms(): pl.pallas_call(kernel, out_shape=jax.ShapeDtypeStruct((n, rows, jw), F32)...]
    unnamed x27 -> x47, local copies, waits for them, and re-layouts: 3.93 us -> 8.34 us
    ppermute x1 -> x2, starting transfers between devices: 4.05 us -> 6.88 us  [the longest x1 4.12 us: body(): lax.ppermute(give, 'core', swap)]
    all_to_all x2, waiting for transfers between devices: 17.8 us -> 15.4 us  [exchange(): return lax.all_to_all(parts, axis, split_axis=0, concat_axis=0, tiled=True)]
  transfers between devices with their start and end apart: 12 -> 13, of which waited for: 5 -> 7; matrix products, arithmetic and copies ran while one was open for 3% -> 1% of each run, Pallas kernels for 12% -> 5%
where the time goes in v2:
time: 193 us; the launch traced here: 192 us
  blocking collectives  59.7 us (31%)
  starting transfers between devices  53.9 us (28%)
  waiting for transfers between devices  35.1 us (18%)
  Pallas kernels  15.8 us (8%)
  between operations  15 us (8%)
  local copies, waits for them, and re-layouts  10.2 us (5%)
    all_to_all x4, blocking collectives, exchange(): return lax.all_to_all(parts, axis, split_axis=0, concat_axis=0, tiled=True)  59.7 us
    ppermute x7, starting transfers between devices, body(): lax.ppermute(feature, 'y', [(i, (i + k) % columns) for i in range(columns)])  28.4 us
    all_to_all x2, starting transfers between devices, exchange(): return lax.all_to_all(parts, axis, split_axis=0, concat_axis=0, tiled=True)  18.5 us
    all_to_all x2, waiting for transfers between devices, exchange(): return lax.all_to_all(parts, axis, split_axis=0, concat_axis=0, tiled=True)  15.4 us
    ppermute x7, waiting for transfers between devices, body(): lax.ppermute(feature, 'y', [(i, (i + k) % columns) for i in range(columns)])  12.1 us
    unnamed x47, local copies, waits for them, and re-layouts  8.34 us
    all_gather x1, waiting for transfers between devices, body(): weight_rows = lax.all_gather(w_shard, DOM, axis=0, tiled=True)  6.14 us
    ppermute x1, starting transfers between devices, body(): lax.ppermute(give, 'core', swap)  4.12 us
  transfers between devices with their start and end apart: 13, of which 7 were waited for; matrix products, arithmetic and copies ran while one was open for 1% of the time, Pallas kernels for 5%

profile of v2, /device:TPU:1, one launch (start us, length us, event | category | flops | bytes accessed | tf_op | source)
XLA Modules:
  0.0 191.5 jit_solution(10932101589765691787)
XLA Ops:
  8.5 2.4 %pick_blocks.1 = bf16[64,128,128]{2,1,0:T(8,128)(2,1)} custom-call(s32[64]{0:T(128)} %bitcast.29, bf16[4,128,128]{2,1,0:T(8,128)(2,1)} %bitcast.28), custom_call_target="tpu_custom_call" | custom-call | bytes 2097152 | tf_op jit(solution)/shard_map/pick_blocks/pallas_call | solution.py:31
  10.9 15.0 %all-to-all-start = ((bf16[64,128,128]{2,1,0:T(8,128)(2,1)}), bf16[64,128,128]{2,1,0:T(8,128)(2,1)S(1)}, u32[]{:S(2)}, u32[]{:S(2)}) async-start(bf16[64,128,128]{2,1,0:T(8,128)(2,1)} %pick_blocks.1), calls=%async_computation | async-start | bytes 4194304 | tf_op jit(solution)/shard_map/all_to_all | solution.py:182
  26.7 3.2 %collective-permute-start = (bf16[512,128]{1,0:T(8,128)(2,1)S(1)}, bf16[512,128]{1,0:T(8,128)(2,1)S(1)}, u32[]{:S(2)}, u32[]{:S(2)}) collective-permute-start(bf16[512,128]{1,0:T(8,128)(2,1)S(1)} %copy-done.11), channel_id=1, source_target_pairs={{0,1},{1,2},{2,3},{3,4},{4,5},{5,6},{6,7},{7,0},{8,9},{9,10},{10,1... | collective-permute-start | bytes 393224 | tf_op jit(solution)/shard_map/ppermute | solution.py:221
  29.9 4.2 %collective-permute-start.1 = (bf16[512,128]{1,0:T(8,128)(2,1)S(1)}, bf16[512,128]{1,0:T(8,128)(2,1)S(1)}, u32[]{:S(2)}, u32[]{:S(2)}) collective-permute-start(bf16[512,128]{1,0:T(8,128)(2,1)S(1)} %copy-done.11), channel_id=1, source_target_pairs={{0,2},{1,3},{2,4},{3,5},{4,6},{5,7},{6,0},{7,1},{8,10},{9,11},{10,... | collective-permute-start | bytes 393224 | tf_op jit(solution)/shard_map/ppermute | solution.py:221
  34.2 4.6 %collective-permute-start.2 = (bf16[512,128]{1,0:T(8,128)(2,1)S(1)}, bf16[512,128]{1,0:T(8,128)(2,1)S(1)}, u32[]{:S(2)}, u32[]{:S(2)}) collective-permute-start(bf16[512,128]{1,0:T(8,128)(2,1)S(1)} %copy-done.11), channel_id=1, source_target_pairs={{0,3},{1,4},{2,5},{3,6},{4,7},{5,0},{6,1},{7,2},{8,11},{9,12},{10,... | collective-permute-start | bytes 393224 | tf_op jit(solution)/shard_map/ppermute | solution.py:221
  38.8 3.5 %collective-permute-start.3 = (bf16[512,128]{1,0:T(8,128)(2,1)S(1)}, bf16[512,128]{1,0:T(8,128)(2,1)S(1)}, u32[]{:S(2)}, u32[]{:S(2)}) collective-permute-start(bf16[512,128]{1,0:T(8,128)(2,1)S(1)} %copy-done.11), channel_id=1, source_target_pairs={{0,4},{1,5},{2,6},{3,7},{4,0},{5,1},{6,2},{7,3},{8,12},{9,13},{10,... | collective-permute-start | bytes 393224 | tf_op jit(solution)/shard_map/ppermute | solution.py:221
  42.4 4.9 %collective-permute-start.4 = (bf16[512,128]{1,0:T(8,128)(2,1)S(1)}, bf16[512,128]{1,0:T(8,128)(2,1)S(1)}, u32[]{:S(2)}, u32[]{:S(2)}) collective-permute-start(bf16[512,128]{1,0:T(8,128)(2,1)S(1)} %copy-done.11), channel_id=1, source_target_pairs={{0,5},{1,6},{2,7},{3,0},{4,1},{5,2},{6,3},{7,4},{8,13},{9,14},{10,... | collective-permute-start | bytes 393224 | tf_op jit(solution)/shard_map/ppermute | solution.py:221
  47.3 5.0 %collective-permute-start.5 = (bf16[512,128]{1,0:T(8,128)(2,1)S(1)}, bf16[512,128]{1,0:T(8,128)(2,1)S(1)}, u32[]{:S(2)}, u32[]{:S(2)}) collective-permute-start(bf16[512,128]{1,0:T(8,128)(2,1)S(1)} %copy-done.11), channel_id=1, source_target_pairs={{0,6},{1,7},{2,0},{3,1},{4,2},{5,3},{6,4},{7,5},{8,14},{9,15},{10,... | collective-permute-start | bytes 393224 | tf_op jit(solution)/shard_map/ppermute | solution.py:221
  52.3 3.0 %collective-permute-start.6 = (bf16[512,128]{1,0:T(8,128)(2,1)S(1)}, bf16[512,128]{1,0:T(8,128)(2,1)S(1)}, u32[]{:S(2)}, u32[]{:S(2)}) collective-permute-start(bf16[512,128]{1,0:T(8,128)(2,1)S(1)} %copy-done.11), channel_id=1, source_target_pairs={{0,7},{1,0},{2,1},{3,2},{4,3},{5,4},{6,5},{7,6},{8,15},{9,8},{10,9... | collective-permute-start | bytes 393224 | tf_op jit(solution)/shard_map/ppermute | solution.py:221
  55.3 4.7 %collective-permute-done.4.refs_6_ = bf16[512,128]{1,0:T(8,128)(2,1)S(1)} collective-permute-done((bf16[512,128]{1,0:T(8,128)(2,1)S(1)}, bf16[512,128]{1,0:T(8,128)(2,1)S(1)}, u32[]{:S(2)}, u32[]{:S(2)}) %collective-permute-start.4) | collective-permute-done | bytes 131104 | tf_op jit(solution)/shard_map/ppermute | solution.py:221
  60.0 6.2 %collective-permute-done.5.refs_7_ = bf16[512,128]{1,0:T(8,128)(2,1)S(1)} collective-permute-done((bf16[512,128]{1,0:T(8,128)(2,1)S(1)}, bf16[512,128]{1,0:T(8,128)(2,1)S(1)}, u32[]{:S(2)}, u32[]{:S(2)}) %collective-permute-start.5) | collective-permute-done | bytes 131104 | tf_op jit(solution)/shard_map/ppermute | solution.py:221
  68.0 2.6 %flip.1.fa_ref = bf16[1024,512]{1,0:T(8,128)(2,1)} custom-call(s32[1]{0:T(128)} %bitcast.1.refs_0_, bf16[512,128]{1,0:T(8,128)(2,1)} %refs_1_.1, bf16[512,128]{1,0:T(8,128)(2,1)} %copy-done.12, bf16[512,128]{1,0:T(8,128)(2,1)} %copy-done.13, bf16[512,128]{1,0:T(8,128)(2,1)} %copy-done.14, bf16[512,128]{1,0:T(8,128)(2,1)} %copy-done.15, ...), custom_call_target="tpu_custom_call" | custom-call | bytes 2097152 | tf_op jit(solution)/shard_map/flip/pallas_call | solution.py:93
  70.6 2.8 %collective-permute-start.7 = (bf16[1024,512]{1,0:T(8,128)(2,1)}, bf16[1024,512]{1,0:T(8,128)(2,1)}, u32[]{:S(2)}, u32[]{:S(2)}) collective-permute-start(bf16[1024,512]{1,0:T(8,128)(2,1)} %flip.1.fa_ref), channel_id=1, source_target_pairs={{0,8},{8,0},{1,9},{9,1},{2,10},{10,2},{3,11},{11,3},{4,12},{12,4},... | collective-permute-start | bytes 3145736 | tf_op jit(solution)/shard_map/ppermute | solution.py:224
  74.1 2.6 %all-to-all-done.inc_ref = bf16[64,128,128]{2,1,0:T(8,128)(2,1)S(1)} async-done(((bf16[64,128,128]{2,1,0:T(8,128)(2,1)}), bf16[64,128,128]{2,1,0:T(8,128)(2,1)S(1)}, u32[]{:S(2)}, u32[]{:S(2)}) %all-to-all-start) | async-done | bytes 2097184 | tf_op jit(solution)/shard_map/all_to_all | solution.py:182
  79.3 4.1 %collective-permute-start.8 = (bf16[512,512]{1,0:T(8,128)(2,1)S(1)}, bf16[512,512]{1,0:T(8,128)(2,1)S(1)}, u32[]{:S(2)}, u32[]{:S(2)}) collective-permute-start(bf16[512,512]{1,0:T(8,128)(2,1)S(1)} %get-tuple-element.15.give_ref), channel_id=1, source_target_pairs={{0,8},{8,0},{1,9},{9,1},{2,10},{10,2},{3,11},{11,3},{4,12},{12,4},... | collective-permute-start | bytes 1572872 | tf_op jit(solution)/shard_map/ppermute | solution.py:236
  84.9 2.7 %weight_terms.1 = bf16[4,1024,128]{2,1,0:T(8,128)(2,1)S(1)} custom-call(bf16[1024,512]{1,0:T(8,128)(2,1)S(1)} %copy-done.1, bf16[1024,512]{1,0:T(8,128)(2,1)} %collective-permute-done.7.fb_ref, bf16[512,512]{1,0:T(8,128)(2,1)S(1)} %get-tuple-element.14.ga_ref.keep_ref, bf16[512,512]{1,0:T(8,128)(2,1)S(1)} %collective-permute-done.8.gb_ref), custom_call_target="tpu_custom_call" | custom-call | flops 1073741824 | bytes 4194304 | tf_op jit(solution)/shard_map/weight_terms/pallas_call | solution.py:139
  87.7 21.7 %all_to_all.30.in_ref = bf16[4,1024,128]{2,1,0:T(8,128)(2,1)} all-to-all(bf16[4,1024,128]{2,1,0:T(8,128)(2,1)S(1)} %weight_terms.1), channel_id=1, replica_groups=mesh['z'=8,'x'=4,'core'=2,'y'=8] {'x'}, dimensions={0} | all-to-all | bytes 2097152 | tf_op jit(solution)/shard_map/all_to_all | solution.py:182
  111.4 6.1 %all-gather.2.cloned.1.call-done.w_ref = bf16[1024,1024]{1,0:T(8,128)(2,1)} async-done(((bf16[16,1024]{1,0:T(8,128)(2,1)}), bf16[1024,1024]{1,0:T(8,128)(2,1)}) %all-gather.2.cloned.1.call-update) | async-done | bytes 2097168 | tf_op jit(solution)/shard_map/all_gather | solution.py:217
  120.2 3.0 %feature_terms.1 = f32[8,512,128]{2,1,0:T(8,128)} custom-call(s32[1]{0:T(128)} %bitcast.core_ref, bf16[512,512]{1,0:T(8,128)(2,1)S(1)} %copy-done.4, bf16[512,512]{1,0:T(8,128)(2,1)S(1)} %copy-done.7, bf16[1024,1024]{1,0:T(8,128)(2,1)S(1)} %copy-done.2), custom_call_target="tpu_custom_call" | custom-call | flops 1073741824 | bytes 4194304 | tf_op jit(solution)/shard_map/feature_terms/pallas_call | solution.py:164
  124.2 15.7 %all_to_all.31.in_ref = bf16[8,128,128]{2,1,0:T(8,128)(2,1)} all-to-all(bf16[8,128,128]{2,1,0:T(8,128)(2,1)S(1)} %bitcast.26), channel_id=1, replica_groups=mesh['z'=8,'x'=4,'core'=2,'y'=8] {'z'}, dimensions={0} | all-to-all | bytes 524288 | tf_op jit(solution)/shard_map/all_to_all | solution.py:182
  141.5 14.0 %all_to_all.32 = bf16[8,128,128]{2,1,0:T(8,128)(2,1)S(1)} all-to-all(bf16[8,128,128]{2,1,0:T(8,128)(2,1)} %fold.3), channel_id=1, replica_groups=mesh['z'=8,'x'=4,'core'=2,'y'=8] {'z'}, dimensions={0} | all-to-all | bytes 524288 | tf_op jit(solution)/shard_map/all_to_all | solution.py:182
  156.7 3.5 %all-to-all-start.4 = ((bf16[4,1024,128]{2,1,0:T(8,128)(2,1)}), bf16[4,1024,128]{2,1,0:T(8,128)(2,1)S(1)}, u32[]{:S(2)}, u32[]{:S(2)}) async-start(bf16[4,1024,128]{2,1,0:T(8,128)(2,1)} %broadcast_in_dim.78), calls=%async_computation.5 | async-start | bytes 2097152 | tf_op jit(solution)/shard_map/all_to_all | solution.py:182
  160.2 12.8 %all-to-all-done.4 = bf16[4,1024,128]{2,1,0:T(8,128)(2,1)S(1)} async-done(((bf16[4,1024,128]{2,1,0:T(8,128)(2,1)}), bf16[4,1024,128]{2,1,0:T(8,128)(2,1)S(1)}, u32[]{:S(2)}, u32[]{:S(2)}) %all-to-all-start.4) | async-done | bytes 1048608 | tf_op jit(solution)/shard_map/all_to_all | solution.py:182
  173.2 8.4 %all_to_all.33 = bf16[2,4096,128]{2,1,0:T(8,128)(2,1)S(1)} all-to-all(bf16[2,4096,128]{2,1,0:T(8,128)(2,1)S(1)} %broadcast_in_dim.80), channel_id=1, replica_groups=mesh['z'=8,'x'=4,'core'=2,'y'=8] {'core'}, dimensions={0} | all-to-all | bytes 4194304 | tf_op jit(solution)/shard_map/all_to_all | solution.py:182
  (69 shorter events, 19.8 us)
Async XLA Ops:
  10.9 15.8 %copy-start.11 = (bf16[512,128]{1,0:T(8,128)(2,1)S(1)}, bf16[512,128]{1,0:T(8,128)(2,1)}, u32[]{:S(2)}) copy-start(bf16[512,128]{1,0:T(8,128)(2,1)} %refs_1_.1) | copy-start | bytes 393220
  10.9 65.8 %all-to-all-start = ((bf16[64,128,128]{2,1,0:T(8,128)(2,1)}), bf16[64,128,128]{2,1,0:T(8,128)(2,1)S(1)}, u32[]{:S(2)}, u32[]{:S(2)}) async-start(bf16[64,128,128]{2,1,0:T(8,128)(2,1)} %pick_blocks.1), calls=%async_computation | async-start | bytes 4194304 | tf_op jit(solution)/shard_map/all_to_all | solution.py:182
  25.9 48.2 %copy-start.21 = (s32[32]{0:T(128)S(1)}, s32[32]{0:T(128)}, u32[]{:S(2)}) copy-start(s32[32]{0:T(128)} %param.18) | copy-start | bytes 388
  25.9 48.2 %copy-start.22 = (s32[32]{0:T(128)S(1)}, s32[32]{0:T(128)}, u32[]{:S(2)}) copy-start(s32[32]{0:T(128)} %param.17) | copy-start | bytes 388
  25.9 50.8 %copy-start.8 = (s32[32]{0:T(128)S(1)}, s32[32]{0:T(128)}, u32[]{:S(2)}) copy-start(s32[32]{0:T(128)} %peer_ref.1) | copy-start | bytes 388
  25.9 91.6 %all-gather.2.cloned.1.call-start = ((), (), s32[]{:S(2)}) async-start(), calls=%async_computation.7 | async-start | bytes 2129920 | tf_op jit(solution)/shard_map/all_gather | solution.py:217
  26.7 154.9 %reduce-scatter.2.cloned.1.call-start = ((), (), s32[]{:S(2)}) async-start(), calls=%async_computation.8 | async-start | bytes 2359296 | tf_op jit(solution)/shard_map/reduce_scatter | solution.py:248
  26.7 20.5 %collective-permute-start = (bf16[512,128]{1,0:T(8,128)(2,1)S(1)}, bf16[512,128]{1,0:T(8,128)(2,1)S(1)}, u32[]{:S(2)}, u32[]{:S(2)}) collective-permute-start(bf16[512,128]{1,0:T(8,128)(2,1)S(1)} %copy-done.11), channel_id=1, source_target_pairs={{0,1},{1,2},{2,3},{3,4},{4,5},{5,6},{6,7},{7,0},{8,9},{9,10},{10,1... | collective-permute-start | bytes 393224 | tf_op jit(solution)/shard_map/ppermute | solution.py:221
  29.9 22.3 %collective-permute-start.1 = (bf16[512,128]{1,0:T(8,128)(2,1)S(1)}, bf16[512,128]{1,0:T(8,128)(2,1)S(1)}, u32[]{:S(2)}, u32[]{:S(2)}) collective-permute-start(bf16[512,128]{1,0:T(8,128)(2,1)S(1)} %copy-done.11), channel_id=1, source_target_pairs={{0,2},{1,3},{2,4},{3,5},{4,6},{5,7},{6,0},{7,1},{8,10},{9,11},{10,... | collective-permute-start | bytes 393224 | tf_op jit(solution)/shard_map/ppermute | solution.py:221
  34.2 21.1 %collective-permute-start.2 = (bf16[512,128]{1,0:T(8,128)(2,1)S(1)}, bf16[512,128]{1,0:T(8,128)(2,1)S(1)}, u32[]{:S(2)}, u32[]{:S(2)}) collective-permute-start(bf16[512,128]{1,0:T(8,128)(2,1)S(1)} %copy-done.11), channel_id=1, source_target_pairs={{0,3},{1,4},{2,5},{3,6},{4,7},{5,0},{6,1},{7,2},{8,11},{9,12},{10,... | collective-permute-start | bytes 393224 | tf_op jit(solution)/shard_map/ppermute | solution.py:221
  38.8 16.5 %collective-permute-start.3 = (bf16[512,128]{1,0:T(8,128)(2,1)S(1)}, bf16[512,128]{1,0:T(8,128)(2,1)S(1)}, u32[]{:S(2)}, u32[]{:S(2)}) collective-permute-start(bf16[512,128]{1,0:T(8,128)(2,1)S(1)} %copy-done.11), channel_id=1, source_target_pairs={{0,4},{1,5},{2,6},{3,7},{4,0},{5,1},{6,2},{7,3},{8,12},{9,13},{10,... | collective-permute-start | bytes 393224 | tf_op jit(solution)/shard_map/ppermute | solution.py:221
  42.4 17.6 %collective-permute-start.4 = (bf16[512,128]{1,0:T(8,128)(2,1)S(1)}, bf16[512,128]{1,0:T(8,128)(2,1)S(1)}, u32[]{:S(2)}, u32[]{:S(2)}) collective-permute-start(bf16[512,128]{1,0:T(8,128)(2,1)S(1)} %copy-done.11), channel_id=1, source_target_pairs={{0,5},{1,6},{2,7},{3,0},{4,1},{5,2},{6,3},{7,4},{8,13},{9,14},{10,... | collective-permute-start | bytes 393224 | tf_op jit(solution)/shard_map/ppermute | solution.py:221
  47.2 20.1 %copy-start.12 = (bf16[512,128]{1,0:T(8,128)(2,1)}, bf16[512,128]{1,0:T(8,128)(2,1)S(1)}, u32[]{:S(2)}) copy-start(bf16[512,128]{1,0:T(8,128)(2,1)S(1)} %collective-permute-done.refs_2_) | copy-start | bytes 393220
  47.3 18.9 %collective-permute-start.5 = (bf16[512,128]{1,0:T(8,128)(2,1)S(1)}, bf16[512,128]{1,0:T(8,128)(2,1)S(1)}, u32[]{:S(2)}, u32[]{:S(2)}) collective-permute-start(bf16[512,128]{1,0:T(8,128)(2,1)S(1)} %copy-done.11), channel_id=1, source_target_pairs={{0,6},{1,7},{2,0},{3,1},{4,2},{5,3},{6,4},{7,5},{8,14},{9,15},{10,... | collective-permute-start | bytes 393224 | tf_op jit(solution)/shard_map/ppermute | solution.py:221
  52.2 15.1 %copy-start.13 = (bf16[512,128]{1,0:T(8,128)(2,1)}, bf16[512,128]{1,0:T(8,128)(2,1)S(1)}, u32[]{:S(2)}) copy-start(bf16[512,128]{1,0:T(8,128)(2,1)S(1)} %collective-permute-done.1.refs_3_) | copy-start | bytes 393220
  52.3 15.1 %collective-permute-start.6 = (bf16[512,128]{1,0:T(8,128)(2,1)S(1)}, bf16[512,128]{1,0:T(8,128)(2,1)S(1)}, u32[]{:S(2)}, u32[]{:S(2)}) collective-permute-start(bf16[512,128]{1,0:T(8,128)(2,1)S(1)} %copy-done.11), channel_id=1, source_target_pairs={{0,7},{1,0},{2,1},{3,2},{4,3},{5,4},{6,5},{7,6},{8,15},{9,8},{10,9... | collective-permute-start | bytes 393224 | tf_op jit(solution)/shard_map/ppermute | solution.py:221
  55.3 12.1 %copy-start.14 = (bf16[512,128]{1,0:T(8,128)(2,1)}, bf16[512,128]{1,0:T(8,128)(2,1)S(1)}, u32[]{:S(2)}) copy-start(bf16[512,128]{1,0:T(8,128)(2,1)S(1)} %collective-permute-done.2.refs_4_) | copy-start | bytes 393220
  70.6 14.3 %copy-start.1 = (bf16[1024,512]{1,0:T(8,128)(2,1)S(1)}, bf16[1024,512]{1,0:T(8,128)(2,1)}, u32[]{:S(2)}) copy-start(bf16[1024,512]{1,0:T(8,128)(2,1)} %flip.1.fa_ref) | copy-start | bytes 3145732
  70.6 13.6 %collective-permute-start.7 = (bf16[1024,512]{1,0:T(8,128)(2,1)}, bf16[1024,512]{1,0:T(8,128)(2,1)}, u32[]{:S(2)}, u32[]{:S(2)}) collective-permute-start(bf16[1024,512]{1,0:T(8,128)(2,1)} %flip.1.fa_ref), channel_id=1, source_target_pairs={{0,8},{8,0},{1,9},{9,1},{2,10},{10,2},{3,11},{11,3},{4,12},{12,4},... | collective-permute-start | bytes 3145736 | tf_op jit(solution)/shard_map/ppermute | solution.py:224
  79.3 5.6 %collective-permute-start.8 = (bf16[512,512]{1,0:T(8,128)(2,1)S(1)}, bf16[512,512]{1,0:T(8,128)(2,1)S(1)}, u32[]{:S(2)}, u32[]{:S(2)}) collective-permute-start(bf16[512,512]{1,0:T(8,128)(2,1)S(1)} %get-tuple-element.15.give_ref), channel_id=1, source_target_pairs={{0,8},{8,0},{1,9},{9,1},{2,10},{10,2},{3,11},{11,3},{4,12},{12,4},... | collective-permute-start | bytes 1572872 | tf_op jit(solution)/shard_map/ppermute | solution.py:236
  87.7 29.9 %copy-start.7 = (bf16[512,512]{1,0:T(8,128)(2,1)S(1)}, bf16[512,512]{1,0:T(8,128)(2,1)}, u32[]{:S(2)}) copy-start(bf16[512,512]{1,0:T(8,128)(2,1)} %copy-done.6) | copy-start | bytes 1572868
  141.5 18.7 %copy-start.19 = (s32[512]{0:T(512)S(1)}, s32[512]{0:T(512)}, u32[]{:S(2)}) copy-start(s32[512]{0:T(512)} %param.13) | copy-start | bytes 6148
  141.5 18.7 %copy-start.20 = (f32[3,128]{1,0:T(4,128)S(1)}, f32[3,128]{1,0:T(4,128)}, u32[]{:S(2)}) copy-start(f32[3,128]{1,0:T(4,128)} %param.14) | copy-start | bytes 4612
  156.7 16.3 %all-to-all-start.4 = ((bf16[4,1024,128]{2,1,0:T(8,128)(2,1)}), bf16[4,1024,128]{2,1,0:T(8,128)(2,1)S(1)}, u32[]{:S(2)}, u32[]{:S(2)}) async-start(bf16[4,1024,128]{2,1,0:T(8,128)(2,1)} %broadcast_in_dim.78), calls=%async_computation.5 | async-start | bytes 2097152 | tf_op jit(solution)/shard_map/all_to_all | solution.py:182
  (12 other events, 44.6 us)
Sparse Core Ops, SparseCore 0:
  30.1 87.3 all-gather.1
  123.4 36.8 reduce-scatter.1

commit v3 on v2

--- a/solution.py
+++ b/solution.py
@@ -74,30 +74,92 @@
             pltpu.VMEM((slots, size, cols), F32),
             pltpu.VMEM((buckets + 1, size, cols), F32),
         ],
-        compiler_params=pltpu.CompilerParams(vmem_limit_bytes=24 << 20),
+        compiler_params=pltpu.CompilerParams(vmem_limit_bytes=12 << 20),
         cost_estimate=cost(2 * slots * size * size * cols, 4 << 20),
         name="merge_tiles",
     )(core, peer, slot, count, tiles, incoming)
 
 
 def flip(column, pieces):
-    n = len(pieces)
-    rows, cols = pieces[0].shape
+    n = sum(p.shape[0] for p in pieces)
+    _, rows, cols = pieces[0].shape
 
     def kernel(*refs):
-        col_ref, out_ref = refs[0], refs[n + 1]
-        for k in range(n):
-            at = lax.rem(col_ref[0] - k + n, n)
-            out_ref[pl.ds(pl.multiple_of(at * cols, cols), cols), :] = refs[k + 1][...].T
+        col_ref, out_ref = refs[0], refs[-1]
+        k = 0
+        for ref in refs[1:-1]:
+            for i in range(ref.shape[0]):
+                at = jnp.bitwise_xor(col_ref[0], turned(k, n))
+                out_ref[pl.ds(pl.multiple_of(at * cols, cols), cols), :] = ref[i].T
+                k += 1
 
     return pl.pallas_call(
         kernel,
         out_shape=jax.ShapeDtypeStruct((n * cols, rows), pieces[0].dtype),
-        in_specs=[pl.BlockSpec(memory_space=pltpu.SMEM)] + [whole()] * n,
+        in_specs=[pl.BlockSpec(memory_space=pltpu.SMEM)] + [whole()] * len(pieces),
         out_specs=whole(),
+        compiler_params=pltpu.CompilerParams(vmem_limit_bytes=8 << 20),
         cost_estimate=cost(0, 2 * n * rows * cols * 2),
         name="flip",
     )(column, *pieces)
+
+
+def turned(k, n):
+    out, bit = 0, n // 2
+    while bit:
+        out += bit * (k % 2)
+        k //= 2
+        bit //= 2
+    return out
+
+
+def double(part, axis):
+    n = lax.axis_size(axis)
+    held, pieces, step = part[None], [part[None]], n // 2
+    while step:
+        got = lax.ppermute(held, axis, [(i, i ^ step) for i in range(n)])
+        pieces.append(got)
+        step //= 2
+        if step:
+            held = jnp.concatenate([held, got], axis=0)
+    return pieces
+
+
+def place(core, mine, other):
+    rows, cols = mine.shape
+    smem = pl.BlockSpec(memory_space=pltpu.SMEM)
+    anywhere = pl.BlockSpec(memory_space=pl.ANY)
+
+    def put(at_ref, part_ref, out_ref, sem):
+        copy = pltpu.make_async_copy(part_ref, out_ref.at[at_ref[0]], sem)
+        copy.start()
+        copy.wait()
+
+    def put_into(at_ref, part_ref, _, out_ref, sem):
+        put(at_ref, part_ref, out_ref, sem)
+
+    shape = jax.ShapeDtypeStruct((2, rows, cols), mine.dtype)
+    half = pl.pallas_call(
+        put,
+        out_shape=shape,
+        in_specs=[smem, whole()],
+        out_specs=anywhere,
+        scratch_shapes=[pltpu.SemaphoreType.DMA],
+        compiler_params=pltpu.CompilerParams(vmem_limit_bytes=4 << 20),
+        cost_estimate=cost(0, 2 * rows * cols * 2),
+        name="place",
+    )(core, mine)
+    return pl.pallas_call(
+        put_into,
+        out_shape=shape,
+        in_specs=[smem, whole(), anywhere],
+        out_specs=anywhere,
+        input_output_aliases={2: 0},
+        scratch_shapes=[pltpu.SemaphoreType.DMA],
+        compiler_params=pltpu.CompilerParams(vmem_limit_bytes=4 << 20),
+        cost_estimate=cost(0, 2 * rows * cols * 2),
+        name="place_into",
+    )(1 - core, other, half)
 
 
 def fold(parts, scale, copies):
@@ -118,6 +180,7 @@
         out_shape=jax.ShapeDtypeStruct((copies, rows, cols), BF),
         in_specs=[whole()],
         out_specs=whole(),
+        compiler_params=pltpu.CompilerParams(vmem_limit_bytes=8 << 20),
         cost_estimate=cost(n * rows * cols, (n + copies) * rows * cols * 2),
         name="fold",
     )(parts)
@@ -142,24 +205,29 @@
         grid=(half // group,),
         in_specs=[whole(), whole(), grad_spec, grad_spec],
         out_specs=pl.BlockSpec((group, features, cols), lambda i: (i, 0, 0)),
-        compiler_params=pltpu.CompilerParams(vmem_limit_bytes=24 << 20),
+        compiler_params=pltpu.CompilerParams(vmem_limit_bytes=12 << 20),
         cost_estimate=cost(4 * features * rows * wide, 4 << 20),
         name="weight_terms",
     )(own_t, other_t, own_grad, other_grad)
 
 
-def feature_terms(core, keep, give, weight_rows, n):
+def feature_terms(core, keep, give, shards, n):
     rows, wide = keep.shape
-    jw = weight_rows.shape[0] // n
+    partitions, relations, w_rows, cols = shards.shape
+    jw = partitions * w_rows // n
     group = 2
-
-    def kernel(core_ref, keep_ref, give_ref, w_ref, out_ref):
+    each = partitions * group // n
+
+    def kernel(core_ref, keep_ref, give_ref, w_ref, out_ref, w_all):
+        for p in range(each):
+            for r in range(relations):
+                w_all[p * w_rows : (p + 1) * w_rows, r * cols : (r + 1) * cols] = w_ref[p, r]
         first = pl.multiple_of(core_ref[0] * wide, wide)
         dims = (((1,), (1,)), ((), ()))
-        d = lax.dot_general(keep_ref[...], w_ref[:, pl.ds(first, wide)], dims, preferred_element_type=F32)
-        d = d + lax.dot_general(give_ref[...], w_ref[:, pl.ds(wide - first, wide)], dims, preferred_element_type=F32)
-        for c in range(group):
-            out_ref[c] = d[:, c * jw : (c + 1) * jw]
+        d = lax.dot_general(keep_ref[...], w_all[:, pl.ds(first, wide)], dims, preferred_element_type=F32)
+        d = d + lax.dot_general(give_ref[...], w_all[:, pl.ds(wide - first, wide)], dims, preferred_element_type=F32)
+        for g in range(group):
+            out_ref[g] = d[:, g * jw : (g + 1) * jw]
 
     return pl.pallas_call(
         kernel,
@@ -169,13 +237,14 @@
             pl.BlockSpec(memory_space=pltpu.SMEM),
             whole(),
             whole(),
-            pl.BlockSpec((group * jw, 2 * wide), lambda c: (c, 0)),
+            pl.BlockSpec((each, relations, w_rows, cols), lambda c: (c, 0, 0, 0)),
         ],
         out_specs=pl.BlockSpec((group, rows, jw), lambda c: (c, 0, 0)),
-        compiler_params=pltpu.CompilerParams(vmem_limit_bytes=24 << 20),
+        scratch_shapes=[pltpu.VMEM((group * jw, 2 * wide), BF)],
+        compiler_params=pltpu.CompilerParams(vmem_limit_bytes=12 << 20),
         cost_estimate=cost(4 * n * jw * rows * wide, 4 << 20),
         name="feature_terms",
-    )(core, keep, give, weight_rows)
+    )(core, keep, give, shards)
 
 
 def exchange(parts, axis):
@@ -203,7 +272,7 @@
     row_count, col_width = cotangent.shape
     tile_size = tile_values.shape[1]
     block_count = row_count // tile_size
-    relations, w_rows, _ = weights.shape
+    relations = weights.shape[0]
     half = relations // 2
     columns = lax.axis_size("y")
     nx = lax.axis_size("x")
@@ -212,14 +281,10 @@
     column = lax.axis_index("y").astype(jnp.int32)[None]
     swap = [(0, 1), (1, 0)]
 
-    w_shard = weights.transpose(1, 0, 2).reshape(w_rows, relations * col_width)
-    w_shard, wanted = lax.optimization_barrier((w_shard, send_block[0]))
-    weight_rows = lax.all_gather(w_shard, DOM, axis=0, tiled=True)
-    outgoing = pick_blocks(wanted, cotangent.reshape(block_count, tile_size, col_width))
+    shards = lax.all_gather(weights, DOM, axis=0)
+    outgoing = pick_blocks(send_block[0], cotangent.reshape(block_count, tile_size, col_width))
     incoming = exchange(outgoing, DOM)
-    pieces = [feature] + [
-        lax.ppermute(feature, "y", [(i, (i + k) % columns) for i in range(columns)]) for k in range(1, columns)
-    ]
+    pieces = double(feature, "y")
     own_t = flip(column, pieces)
     other_t = lax.ppermute(own_t, "core", swap)
     keep, give = merge_tiles(
@@ -237,15 +302,17 @@
     j_count = mine.shape[1]
     mine = mine.reshape(nx, half * j_count // nx, col_width)
     mine = fold(exchange(mine, "x"), None, 1)
-    mine, late_keep, late_give, late_rows = lax.optimization_barrier((mine, keep, give, weight_rows))
+    mine, keep, give = lax.optimization_barrier((mine, keep, give))
+    partial = feature_terms(core, keep, give, shards, columns)
+    mine, partial = lax.optimization_barrier((exchange(mine.reshape(nz, -1, col_width), "z"), partial))
+    partial = lax.psum_scatter(partial, "y", scatter_dimension=0, tiled=True)[0]
     norm_scale = 1.0 / math.sqrt(row_count * partitions)
-    mine = fold(exchange(mine.reshape(nz, -1, col_width), "z"), norm_scale, nz)
+    mine = fold(mine, norm_scale, nz)
     mine = exchange(mine, "z").reshape(-1, col_width)
     mine = exchange(repeat(mine, nx), "x").reshape(-1, col_width)
-    weight_grad = exchange(repeat(mine, 2), "core").reshape(relations, j_count, col_width)
-
-    partial = feature_terms(core, late_keep, late_give, late_rows, columns)
-    partial = lax.psum_scatter(partial, "y", scatter_dimension=0, tiled=True)[0]
+
+    weight_grad = place(core, mine, lax.ppermute(mine, "core", swap)).reshape(relations, j_count, col_width)
+
     kind = node_type[:, None]
     gains = jnp.where(kind == 0, self_gain[0:1], jnp.where(kind == 1, self_gain[1:2], self_gain[2:3]))
     self_term = cotangent.astype(F32) * gains

time: 193 us -> 174 us (0.902)
  the two profiles are of different devices: /device:TPU:1 before, /device:TPU:2 now
where the time goes in v3:
time: 174 us; the launch traced here: 173 us
  blocking collectives  50 us (29%)
  waiting for transfers between devices  43.7 us (25%)
  starting transfers between devices  42.4 us (24%)
  between operations  15 us (9%)
  Pallas kernels  12.8 us (7%)
  local copies, waits for them, and re-layouts  6.6 us (4%)
  other arithmetic  2.75 us (2%)
    all_to_all x3, blocking collectives, exchange(): return lax.all_to_all(parts, axis, split_axis=0, concat_axis=0, tiled=True)  50 us
    ppermute x3, waiting for transfers between devices, double(): got = lax.ppermute(held, axis, [(i, i ^ step) for i in range(n)])  26.9 us
    all_to_all x2, starting transfers between devices, exchange(): return lax.all_to_all(parts, axis, split_axis=0, concat_axis=0, tiled=True)  19.5 us
    ppermute x3, starting transfers between devices, double(): got = lax.ppermute(held, axis, [(i, i ^ step) for i in range(n)])  17 us
    all_to_all x2, waiting for transfers between devices, exchange(): return lax.all_to_all(parts, axis, split_axis=0, concat_axis=0, tiled=True)  6.96 us
    unnamed x34, local copies, waits for them, and re-layouts  6.46 us
    reduce_scatter x1, waiting for transfers between devices, body(): partial = lax.psum_scatter(partial, 'y', scatter_dimension=0, tiled=True)[0]  5.84 us
  transfers between devices with their start and end apart: 10, of which 9 were waited for; matrix products, arithmetic and copies ran while one was open for 1% of the time, Pallas kernels for 6%

profile of v3, /device:TPU:2, one launch (start us, length us, event | category | flops | bytes accessed | tf_op | source)
XLA Modules:
  0.0 173.2 jit_solution(10257446998955908189)
XLA Ops:
  7.2 2.4 %pick_blocks.1 = bf16[64,128,128]{2,1,0:T(8,128)(2,1)} custom-call(s32[64]{0:T(128)} %bitcast.30, bf16[4,128,128]{2,1,0:T(8,128)(2,1)} %bitcast.29), custom_call_target="tpu_custom_call" | custom-call | bytes 2097152 | tf_op jit(solution)/shard_map/pick_blocks/pallas_call | solution.py:31
  9.5 14.0 %all-to-all-start = ((bf16[64,128,128]{2,1,0:T(8,128)(2,1)}), bf16[64,128,128]{2,1,0:T(8,128)(2,1)S(1)}, u32[]{:S(2)}, u32[]{:S(2)}) async-start(bf16[64,128,128]{2,1,0:T(8,128)(2,1)} %pick_blocks.1), calls=%async_computation | async-start | bytes 4194304 | tf_op jit(solution)/shard_map/all_to_all | solution.py:251
  24.3 7.7 %collective-permute-start = (bf16[1,512,128]{2,1,0:T(8,128)(2,1)S(1)}, bf16[1,512,128]{2,1,0:T(8,128)(2,1)S(1)}, u32[]{:S(2)}, u32[]{:S(2)}) collective-permute-start(bf16[1,512,128]{2,1,0:T(8,128)(2,1)S(1)} %bitcast.23), channel_id=1, source_target_pairs={{0,4},{1,5},{2,6},{3,7},{4,0},{5,1},{6,2},{7,3},{8,12},{9,13},{10,... | collective-permute-start | bytes 393224 | tf_op jit(solution)/shard_map/ppermute | solution.py:120
  32.1 3.9 %collective-permute-done.refs_2_ = bf16[1,512,128]{2,1,0:T(8,128)(2,1)S(1)} collective-permute-done((bf16[1,512,128]{2,1,0:T(8,128)(2,1)S(1)}, bf16[1,512,128]{2,1,0:T(8,128)(2,1)S(1)}, u32[]{:S(2)}, u32[]{:S(2)}) %collective-permute-start) | collective-permute-done | bytes 131104 | tf_op jit(solution)/shard_map/ppermute | solution.py:120
  36.0 7.1 %collective-permute-start.1 = (bf16[2,512,128]{2,1,0:T(8,128)(2,1)S(1)}, bf16[2,512,128]{2,1,0:T(8,128)(2,1)S(1)}, u32[]{:S(2)}, u32[]{:S(2)}) collective-permute-start(bf16[2,512,128]{2,1,0:T(8,128)(2,1)S(1)} %pad_maximum_fusion.1), channel_id=1, source_target_pairs={{0,2},{1,3},{2,0},{3,1},{4,6},{5,7},{6,4},{7,5},{8,10},{9,11},{10,... | collective-permute-start | bytes 786440 | tf_op jit(solution)/shard_map/ppermute | solution.py:120
  43.1 9.6 %collective-permute-done.1.refs_3_ = bf16[2,512,128]{2,1,0:T(8,128)(2,1)S(1)} collective-permute-done((bf16[2,512,128]{2,1,0:T(8,128)(2,1)S(1)}, bf16[2,512,128]{2,1,0:T(8,128)(2,1)S(1)}, u32[]{:S(2)}, u32[]{:S(2)}) %collective-permute-start.1) | collective-permute-done | bytes 262176 | tf_op jit(solution)/shard_map/ppermute | solution.py:120
  53.6 2.2 %collective-permute-start.2 = (bf16[4,512,128]{2,1,0:T(8,128)(2,1)}, bf16[4,512,128]{2,1,0:T(8,128)(2,1)S(1)}, u32[]{:S(2)}, u32[]{:S(2)}) collective-permute-start(bf16[4,512,128]{2,1,0:T(8,128)(2,1)} %pad_maximum_fusion), channel_id=1, source_target_pairs={{0,1},{1,0},{2,3},{3,2},{4,5},{5,4},{6,7},{7,6},{8,9},{9,8},{10,11... | collective-permute-start | bytes 1572872 | tf_op jit(solution)/shard_map/ppermute | solution.py:120
  55.8 13.5 %collective-permute-done.2.refs_4_ = bf16[4,512,128]{2,1,0:T(8,128)(2,1)S(1)} collective-permute-done((bf16[4,512,128]{2,1,0:T(8,128)(2,1)}, bf16[4,512,128]{2,1,0:T(8,128)(2,1)S(1)}, u32[]{:S(2)}, u32[]{:S(2)}) %collective-permute-start.2) | collective-permute-done | bytes 524320 | tf_op jit(solution)/shard_map/ppermute | solution.py:120
  72.4 1.9 %collective-permute-start.3 = (bf16[1024,512]{1,0:T(8,128)(2,1)S(1)}, bf16[1024,512]{1,0:T(8,128)(2,1)}, u32[]{:S(2)}, u32[]{:S(2)}) collective-permute-start(bf16[1024,512]{1,0:T(8,128)(2,1)S(1)} %flip.1.fa_ref), channel_id=1, source_target_pairs={{0,8},{8,0},{1,9},{9,1},{2,10},{10,2},{3,11},{11,3},{4,12},{12,4},... | collective-permute-start | bytes 3145736 | tf_op jit(solution)/shard_map/ppermute | solution.py:289
  76.0 1.2 copy-done.6
  77.3 1.3 merge_tiles.1
  78.6 1.9 %collective-permute-start.4 = (bf16[512,512]{1,0:T(8,128)(2,1)S(1)}, bf16[512,512]{1,0:T(8,128)(2,1)S(1)}, u32[]{:S(2)}, u32[]{:S(2)}) collective-permute-start(bf16[512,512]{1,0:T(8,128)(2,1)S(1)} %get-tuple-element.13.give_ref), channel_id=1, source_target_pairs={{0,8},{8,0},{1,9},{9,1},{2,10},{10,2},{3,11},{11,3},{4,12},{12,4},... | collective-permute-start | bytes 1572872 | tf_op jit(solution)/shard_map/ppermute | solution.py:301
  82.4 2.7 %weight_terms.1 = bf16[4,1024,128]{2,1,0:T(8,128)(2,1)S(1)} custom-call(bf16[1024,512]{1,0:T(8,128)(2,1)S(1)} %flip.1.fa_ref, bf16[1024,512]{1,0:T(8,128)(2,1)} %collective-permute-done.3.fb_ref, bf16[512,512]{1,0:T(8,128)(2,1)S(1)} %get-tuple-element.12.ga_ref.keep_ref, bf16[512,512]{1,0:T(8,128)(2,1)S(1)} %collective-permute-done.4.gb_ref), custom_call_target="tpu_custom_call" | custom-call | flops 1073741824 | bytes 4194304 | tf_op jit(solution)/shard_map/weight_terms/pallas_call | solution.py:202
  85.1 21.5 %all_to_all.25.in_ref = bf16[4,1024,128]{2,1,0:T(8,128)(2,1)S(1)} all-to-all(bf16[4,1024,128]{2,1,0:T(8,128)(2,1)S(1)} %weight_terms.1), channel_id=1, replica_groups=mesh['z'=8,'x'=4,'core'=2,'y'=8] {'x'}, dimensions={0} | all-to-all | bytes 2097152 | tf_op jit(solution)/shard_map/all_to_all | solution.py:251
  107.5 5.5 %all-to-all-start.2 = ((bf16[8,128,128]{2,1,0:T(8,128)(2,1)}), bf16[8,128,128]{2,1,0:T(8,128)(2,1)S(1)}, u32[]{:S(2)}, u32[]{:S(2)}) async-start(bf16[8,128,128]{2,1,0:T(8,128)(2,1)} %bitcast.5), calls=%async_computation.2 | async-start | bytes 524288 | tf_op jit(solution)/shard_map/all_to_all | solution.py:251
  113.7 1.6 copy-done
  115.3 3.3 %feature_terms.1 = f32[8,512,128]{2,1,0:T(8,128)} custom-call(s32[1]{0:T(128)} %bitcast.2.core_ref.at_ref, bf16[512,512]{1,0:T(8,128)(2,1)S(1)} %copy-done.2, bf16[512,512]{1,0:T(8,128)(2,1)S(1)} %copy-done.10, bf16[64,8,16,128]{3,2,1,0:T(8,128)(2,1)S(1)} %bitcast.22), custom_call_target="tpu_custom_call" | custom-call | flops 1073741824 | bytes 4194304 | tf_op jit(solution)/shard_map/feature_terms/pallas_call | solution.py:232
  118.5 5.9 %all-to-all-done.2.in_ref = bf16[8,128,128]{2,1,0:T(8,128)(2,1)S(1)} async-done(((bf16[8,128,128]{2,1,0:T(8,128)(2,1)}), bf16[8,128,128]{2,1,0:T(8,128)(2,1)S(1)}, u32[]{:S(2)}, u32[]{:S(2)}) %all-to-all-start.2) | async-done | bytes 262176 | tf_op jit(solution)/shard_map/all_to_all | solution.py:251
  124.6 12.9 %all_to_all.26 = bf16[8,128,128]{2,1,0:T(8,128)(2,1)S(1)} all-to-all(bf16[8,128,128]{2,1,0:T(8,128)(2,1)S(1)} %fold.3), channel_id=1, replica_groups=mesh['z'=8,'x'=4,'core'=2,'y'=8] {'z'}, dimensions={0} | all-to-all | bytes 524288 | tf_op jit(solution)/shard_map/all_to_all | solution.py:251
  137.6 15.6 %all_to_all.27 = bf16[4,1024,128]{2,1,0:T(8,128)(2,1)S(1)} all-to-all(bf16[4,1024,128]{2,1,0:T(8,128)(2,1)S(1)} %broadcast_in_dim.76), channel_id=1, replica_groups=mesh['z'=8,'x'=4,'core'=2,'y'=8] {'x'}, dimensions={0} | all-to-all | bytes 2097152 | tf_op jit(solution)/shard_map/all_to_all | solution.py:251
  153.2 1.9 %collective-permute-start.5 = (bf16[4096,128]{1,0:T(8,128)(2,1)S(1)}, bf16[4096,128]{1,0:T(8,128)(2,1)S(1)}, u32[]{:S(2)}, u32[]{:S(2)}) collective-permute-start(bf16[4096,128]{1,0:T(8,128)(2,1)S(1)} %bitcast.20), channel_id=1, source_target_pairs={{0,8},{8,0},{1,9},{9,1},{2,10},{10,2},{3,11},{11,3},{4,12},{12,4},... | collective-permute-start | bytes 3145736 | tf_op jit(solution)/shard_map/ppermute | solution.py:314
  156.1 1.6 collective-permute-done.5.part_ref
  158.7 5.8 %reduce-scatter.2.cloned.1.call-done = f32[1,512,128]{2,1,0:T(8,128)} async-done(((f32[8,512,128]{2,1,0:T(8,128)}), f32[1,512,128]{2,1,0:T(8,128)}) %reduce-scatter.2.cloned.1.call-update) | async-done | bytes 262160 | tf_op jit(solution)/shard_map/reduce_scatter | solution.py:308
  164.5 1.8 %fusion = bf16[512,128]{1,0:T(8,128)(2,1)} fusion(f32[1,512,128]{2,1,0:T(8,128)} %reduce-scatter.2.cloned.1.call-done, bf16[512,128]{1,0:T(8,128)(2,1)S(1)} %copy-done.12, f32[128]{0:T(128)S(1)} %get-tuple-element.19, f32[128]{0:T(128)S(1)} %get-tuple-element.20, f32[128]{0:T(128)S(1)} %get-tuple-element.18, pred[512]{0:T(512)(128)(4,1)S(1)} %get-tuple-element.17, ...), kind=kLoop, calls=%fused_computation.3 | loop fusion | flops 393216 | bytes 526848 | tf_op jit(solution)/shard_map/convert_element_type | solution.py:319
  (51 shorter events, 11.4 us)
Async XLA Ops:
  9.5 14.8 %copy-start.3 = (bf16[512,128]{1,0:T(8,128)(2,1)S(1)}, bf16[512,128]{1,0:T(8,128)(2,1)}, u32[]{:S(2)}) copy-start(bf16[512,128]{1,0:T(8,128)(2,1)} %param.11) | copy-start | bytes 393220
  9.5 66.5 %all-to-all-start = ((bf16[64,128,128]{2,1,0:T(8,128)(2,1)}), bf16[64,128,128]{2,1,0:T(8,128)(2,1)S(1)}, u32[]{:S(2)}, u32[]{:S(2)}) async-start(bf16[64,128,128]{2,1,0:T(8,128)(2,1)} %pick_blocks.1), calls=%async_computation | async-start | bytes 4194304 | tf_op jit(solution)/shard_map/all_to_all | solution.py:251
  23.5 51.4 %copy-start.15 = (s32[32]{0:T(128)S(1)}, s32[32]{0:T(128)}, u32[]{:S(2)}) copy-start(s32[32]{0:T(128)} %param.18) | copy-start | bytes 388
  23.6 51.4 %copy-start.16 = (s32[32]{0:T(128)S(1)}, s32[32]{0:T(128)}, u32[]{:S(2)}) copy-start(s32[32]{0:T(128)} %param.17) | copy-start | bytes 388
  23.6 52.5 %copy-start.11 = (s32[32]{0:T(128)S(1)}, s32[32]{0:T(128)}, u32[]{:S(2)}) copy-start(s32[32]{0:T(128)} %peer_ref.1) | copy-start | bytes 388
  23.6 90.1 %all-gather.3.cloned.1.call-start = ((), (), s32[]{:S(2)}) async-start(), calls=%async_computation.7 | async-start | bytes 2129920 | tf_op jit(solution)/shard_map/all_gather | solution.py:284
  24.3 11.6 %collective-permute-start = (bf16[1,512,128]{2,1,0:T(8,128)(2,1)S(1)}, bf16[1,512,128]{2,1,0:T(8,128)(2,1)S(1)}, u32[]{:S(2)}, u32[]{:S(2)}) collective-permute-start(bf16[1,512,128]{2,1,0:T(8,128)(2,1)S(1)} %bitcast.23), channel_id=1, source_target_pairs={{0,4},{1,5},{2,6},{3,7},{4,0},{5,1},{6,2},{7,3},{8,12},{9,13},{10,... | collective-permute-start | bytes 393224 | tf_op jit(solution)/shard_map/ppermute | solution.py:120
  36.0 16.7 %collective-permute-start.1 = (bf16[2,512,128]{2,1,0:T(8,128)(2,1)S(1)}, bf16[2,512,128]{2,1,0:T(8,128)(2,1)S(1)}, u32[]{:S(2)}, u32[]{:S(2)}) collective-permute-start(bf16[2,512,128]{2,1,0:T(8,128)(2,1)S(1)} %pad_maximum_fusion.1), channel_id=1, source_target_pairs={{0,2},{1,3},{2,0},{3,1},{4,6},{5,7},{6,4},{7,5},{8,10},{9,11},{10,... | collective-permute-start | bytes 786440 | tf_op jit(solution)/shard_map/ppermute | solution.py:120
  52.7 16.6 %copy-start.4 = (bf16[2,512,128]{2,1,0:T(8,128)(2,1)}, bf16[2,512,128]{2,1,0:T(8,128)(2,1)S(1)}, u32[]{:S(2)}) copy-start(bf16[2,512,128]{2,1,0:T(8,128)(2,1)S(1)} %collective-permute-done.1.refs_3_) | copy-start | bytes 786436
  53.6 15.7 %collective-permute-start.2 = (bf16[4,512,128]{2,1,0:T(8,128)(2,1)}, bf16[4,512,128]{2,1,0:T(8,128)(2,1)S(1)}, u32[]{:S(2)}, u32[]{:S(2)}) collective-permute-start(bf16[4,512,128]{2,1,0:T(8,128)(2,1)} %pad_maximum_fusion), channel_id=1, source_target_pairs={{0,1},{1,0},{2,3},{3,2},{4,5},{5,4},{6,7},{7,6},{8,9},{9,8},{10,11... | collective-permute-start | bytes 1572872 | tf_op jit(solution)/shard_map/ppermute | solution.py:120
  71.0 1.0 copy-start.8
  72.4 8.9 %collective-permute-start.3 = (bf16[1024,512]{1,0:T(8,128)(2,1)S(1)}, bf16[1024,512]{1,0:T(8,128)(2,1)}, u32[]{:S(2)}, u32[]{:S(2)}) collective-permute-start(bf16[1024,512]{1,0:T(8,128)(2,1)S(1)} %flip.1.fa_ref), channel_id=1, source_target_pairs={{0,8},{8,0},{1,9},{9,1},{2,10},{10,2},{3,11},{11,3},{4,12},{12,4},... | collective-permute-start | bytes 3145736 | tf_op jit(solution)/shard_map/ppermute | solution.py:289
  76.0 1.2 copy-start.6
  78.6 6.6 %copy-start.1 = (bf16[512,512]{1,0:T(8,128)(2,1)}, bf16[512,512]{1,0:T(8,128)(2,1)S(1)}, u32[]{:S(2)}) copy-start(bf16[512,512]{1,0:T(8,128)(2,1)S(1)} %get-tuple-element.12.ga_ref.keep_ref) | copy-start | bytes 1572868
  78.6 3.8 %collective-permute-start.4 = (bf16[512,512]{1,0:T(8,128)(2,1)S(1)}, bf16[512,512]{1,0:T(8,128)(2,1)S(1)}, u32[]{:S(2)}, u32[]{:S(2)}) collective-permute-start(bf16[512,512]{1,0:T(8,128)(2,1)S(1)} %get-tuple-element.13.give_ref), channel_id=1, source_target_pairs={{0,8},{8,0},{1,9},{9,1},{2,10},{10,2},{3,11},{11,3},{4,12},{12,4},... | collective-permute-start | bytes 1572872 | tf_op jit(solution)/shard_map/ppermute | solution.py:301
  85.1 28.5 %copy-start.10 = (bf16[512,512]{1,0:T(8,128)(2,1)S(1)}, bf16[512,512]{1,0:T(8,128)(2,1)}, u32[]{:S(2)}) copy-start(bf16[512,512]{1,0:T(8,128)(2,1)} %copy-done.9) | copy-start | bytes 1572868
  106.6 7.0 %copy-start.2 = (bf16[512,512]{1,0:T(8,128)(2,1)S(1)}, bf16[512,512]{1,0:T(8,128)(2,1)}, u32[]{:S(2)}) copy-start(bf16[512,512]{1,0:T(8,128)(2,1)} %copy-done.1) | copy-start | bytes 1572868
  107.5 17.0 %all-to-all-start.2 = ((bf16[8,128,128]{2,1,0:T(8,128)(2,1)}), bf16[8,128,128]{2,1,0:T(8,128)(2,1)S(1)}, u32[]{:S(2)}, u32[]{:S(2)}) async-start(bf16[8,128,128]{2,1,0:T(8,128)(2,1)} %bitcast.5), calls=%async_computation.2 | async-start | bytes 524288 | tf_op jit(solution)/shard_map/all_to_all | solution.py:251
  113.0 51.6 %reduce-scatter.2.cloned.1.call-start = ((), (), s32[]{:S(2)}) async-start(), calls=%async_computation.6 | async-start | bytes 2359296 | tf_op jit(solution)/shard_map/reduce_scatter | solution.py:308
  113.7 1.6 copy-start
  124.5 30.5 %copy-start.13 = (s32[512]{0:T(512)S(1)}, s32[512]{0:T(512)}, u32[]{:S(2)}) copy-start(s32[512]{0:T(512)} %param.13) | copy-start | bytes 6148
  124.6 30.6 %copy-start.14 = (f32[3,128]{1,0:T(4,128)S(1)}, f32[3,128]{1,0:T(4,128)}, u32[]{:S(2)}) copy-start(f32[3,128]{1,0:T(4,128)} %param.14) | copy-start | bytes 4612
  153.2 4.5 %collective-permute-start.5 = (bf16[4096,128]{1,0:T(8,128)(2,1)S(1)}, bf16[4096,128]{1,0:T(8,128)(2,1)S(1)}, u32[]{:S(2)}, u32[]{:S(2)}) collective-permute-start(bf16[4096,128]{1,0:T(8,128)(2,1)S(1)} %bitcast.20), channel_id=1, source_target_pairs={{0,8},{8,0},{1,9},{9,1},{2,10},{10,2},{3,11},{11,3},{4,12},{12,4},... | collective-permute-start | bytes 3145736 | tf_op jit(solution)/shard_map/ppermute | solution.py:314
  156.1 8.4 %copy-start.12 = (bf16[512,128]{1,0:T(8,128)(2,1)S(1)}, bf16[512,128]{1,0:T(8,128)(2,1)}, u32[]{:S(2)}) copy-start(bf16[512,128]{1,0:T(8,128)(2,1)} %param.12) | copy-start | bytes 393220
  (3 other events, 2.6 us)
Sparse Core Ops, SparseCore 0:
  27.8 85.8 all-gather.2
  124.6 39.8 reduce-scatter.1

commit v4 on v3

--- a/solution.py
+++ b/solution.py
@@ -10,6 +10,7 @@
 BF = jnp.bfloat16
 F32 = jnp.float32
 DOM = ("z", "x", "core")
+PLACE_HINT = 145 * 10**8
 
 
 def cost(flops, nbytes):
@@ -146,7 +147,7 @@
         out_specs=anywhere,
         scratch_shapes=[pltpu.SemaphoreType.DMA],
         compiler_params=pltpu.CompilerParams(vmem_limit_bytes=4 << 20),
-        cost_estimate=cost(0, 2 * rows * cols * 2),
+        cost_estimate=cost(PLACE_HINT, 2 * rows * cols * 2),
         name="place",
     )(core, mine)
     return pl.pallas_call(
@@ -157,15 +158,17 @@
         input_output_aliases={2: 0},
         scratch_shapes=[pltpu.SemaphoreType.DMA],
         compiler_params=pltpu.CompilerParams(vmem_limit_bytes=4 << 20),
-        cost_estimate=cost(0, 2 * rows * cols * 2),
+        cost_estimate=cost(PLACE_HINT, 2 * rows * cols * 2),
         name="place_into",
     )(1 - core, other, half)
 
 
-def fold(parts, scale, copies):
+def fold(parts, scale, copies, after=None):
     n, rows, cols = parts.shape
-
-    def kernel(in_ref, out_ref):
+    marks = [] if after is None else [after]
+
+    def kernel(in_ref, *rest):
+        out_ref = rest[-1]
         total = in_ref[0].astype(F32)
         for i in range(1, n):
             total = total + in_ref[i].astype(F32)
@@ -178,12 +181,12 @@
     return pl.pallas_call(
         kernel,
         out_shape=jax.ShapeDtypeStruct((copies, rows, cols), BF),
-        in_specs=[whole()],
+        in_specs=[whole()] + [pl.BlockSpec(memory_space=pl.ANY)] * len(marks),
         out_specs=whole(),
         compiler_params=pltpu.CompilerParams(vmem_limit_bytes=8 << 20),
         cost_estimate=cost(n * rows * cols, (n + copies) * rows * cols * 2),
         name="fold",
-    )(parts)
+    )(parts, *marks)
 
 
 def weight_terms(own_t, other_t, own_grad, other_grad, half):
@@ -218,7 +221,8 @@
     group = 2
     each = partitions * group // n
 
-    def kernel(core_ref, keep_ref, give_ref, w_ref, out_ref, w_all):
+    def kernel(core_ref, keep_ref, give_ref, w_ref, out_ref, mark_ref, w_all):
+        mark_ref[...] = jnp.zeros_like(mark_ref)
         for p in range(each):
             for r in range(relations):
                 w_all[p * w_rows : (p + 1) * w_rows, r * cols : (r + 1) * cols] = w_ref[p, r]
@@ -231,7 +235,7 @@
 
     return pl.pallas_call(
         kernel,
-        out_shape=jax.ShapeDtypeStruct((n, rows, jw), F32),
+        out_shape=(jax.ShapeDtypeStruct((n, rows, jw), F32), jax.ShapeDtypeStruct((8, 128), F32)),
         grid=(n // group,),
         in_specs=[
             pl.BlockSpec(memory_space=pltpu.SMEM),
@@ -239,7 +243,10 @@
             whole(),
             pl.BlockSpec((each, relations, w_rows, cols), lambda c: (c, 0, 0, 0)),
         ],
-        out_specs=pl.BlockSpec((group, rows, jw), lambda c: (c, 0, 0)),
+        out_specs=(
+            pl.BlockSpec((group, rows, jw), lambda c: (c, 0, 0)),
+            pl.BlockSpec((8, 128), lambda c: (0, 0)),
+        ),
         scratch_shapes=[pltpu.VMEM((group * jw, 2 * wide), BF)],
         compiler_params=pltpu.CompilerParams(vmem_limit_bytes=12 << 20),
         cost_estimate=cost(4 * n * jw * rows * wide, 4 << 20),
@@ -286,6 +293,10 @@
     incoming = exchange(outgoing, DOM)
     pieces = double(feature, "y")
     own_t = flip(column, pieces)
+    kind = node_type[:, None]
+    gains = jnp.where(kind == 0, self_gain[0:1], jnp.where(kind == 1, self_gain[1:2], self_gain[2:3]))
+    self_term = cotangent.astype(F32) * gains
+    own_t, self_term = lax.optimization_barrier((own_t, self_term))
     other_t = lax.ppermute(own_t, "core", swap)
     keep, give = merge_tiles(
         core,
@@ -303,19 +314,15 @@
     mine = mine.reshape(nx, half * j_count // nx, col_width)
     mine = fold(exchange(mine, "x"), None, 1)
     mine, keep, give = lax.optimization_barrier((mine, keep, give))
-    partial = feature_terms(core, keep, give, shards, columns)
-    mine, partial = lax.optimization_barrier((exchange(mine.reshape(nz, -1, col_width), "z"), partial))
+    partial, mark = feature_terms(core, keep, give, shards, columns)
+    mine = exchange(mine.reshape(nz, -1, col_width), "z")
     partial = lax.psum_scatter(partial, "y", scatter_dimension=0, tiled=True)[0]
     norm_scale = 1.0 / math.sqrt(row_count * partitions)
-    mine = fold(mine, norm_scale, nz)
+    mine = fold(mine, norm_scale, nz, mark)
     mine = exchange(mine, "z").reshape(-1, col_width)
     mine = exchange(repeat(mine, nx), "x").reshape(-1, col_width)
-
     weight_grad = place(core, mine, lax.ppermute(mine, "core", swap)).reshape(relations, j_count, col_width)
 
-    kind = node_type[:, None]
-    gains = jnp.where(kind == 0, self_gain[0:1], jnp.where(kind == 1, self_gain[1:2], self_gain[2:3]))
-    self_term = cotangent.astype(F32) * gains
     feature_grad = (partial + self_term).astype(BF)
     return (feature_grad, weight_grad)
 

time: 174 us -> 173 us (level)
  the two profiles are of different devices: /device:TPU:2 before, /device:TPU:1 now
where the time goes in v4:
time: 173 us; the launch traced here: 171 us
  starting transfers between devices  54.5 us (32%)
  waiting for transfers between devices  43.2 us (25%)
  blocking collectives  33.6 us (19%)
  between operations  15 us (9%)
  Pallas kernels  12.8 us (7%)
  local copies, waits for them, and re-layouts  8.6 us (5%)
  other arithmetic  3.48 us (2%)
    all_to_all x2, blocking collectives, exchange(): return lax.all_to_all(parts, axis, split_axis=0, concat_axis=0, tiled=True)  33.6 us
    ppermute x3, waiting for transfers between devices, double(): got = lax.ppermute(held, axis, [(i, i ^ step) for i in range(n)])  24.7 us
    all_to_all x3, starting transfers between devices, exchange(): return lax.all_to_all(parts, axis, split_axis=0, concat_axis=0, tiled=True)  24.2 us
    ppermute x3, starting transfers between devices, double(): got = lax.ppermute(held, axis, [(i, i ^ step) for i in range(n)])  16.8 us
    all_to_all x3, waiting for transfers between devices, exchange(): return lax.all_to_all(parts, axis, split_axis=0, concat_axis=0, tiled=True)  14.5 us
    unnamed x36, local copies, waits for them, and re-layouts  7.49 us
    ppermute x1, starting transfers between devices, body(): lax.ppermute(mine, 'core', swap)  6.46 us
    ppermute x1, starting transfers between devices, body(): other_t = lax.ppermute(own_t, 'core', swap)  3.65 us
  transfers between devices with their start and end apart: 11, of which 8 were waited for; matrix products, arithmetic and copies ran while one was open for 2% of the time, Pallas kernels for 6%

profile of v4, /device:TPU:1, one launch (start us, length us, event | category | flops | bytes accessed | tf_op | source)
XLA Modules:
  0.0 171.2 jit_solution(5474964439289720933)
XLA Ops:
  7.2 2.4 %pick_blocks.1 = bf16[64,128,128]{2,1,0:T(8,128)(2,1)} custom-call(s32[64]{0:T(128)} %bitcast.29, bf16[4,128,128]{2,1,0:T(8,128)(2,1)} %bitcast.28), custom_call_target="tpu_custom_call" | custom-call | bytes 2097152 | tf_op jit(solution)/shard_map/pick_blocks/pallas_call | solution.py:32
  9.6 15.0 %all-to-all-start = ((bf16[64,128,128]{2,1,0:T(8,128)(2,1)}), bf16[64,128,128]{2,1,0:T(8,128)(2,1)S(1)}, u32[]{:S(2)}, u32[]{:S(2)}) async-start(bf16[64,128,128]{2,1,0:T(8,128)(2,1)} %pick_blocks.1), calls=%async_computation | async-start | bytes 4194304 | tf_op jit(solution)/shard_map/all_to_all | solution.py:258
  25.3 7.5 %collective-permute-start = (bf16[1,512,128]{2,1,0:T(8,128)(2,1)S(1)}, bf16[1,512,128]{2,1,0:T(8,128)(2,1)S(1)}, u32[]{:S(2)}, u32[]{:S(2)}) collective-permute-start(bf16[1,512,128]{2,1,0:T(8,128)(2,1)S(1)} %bitcast.20), channel_id=1, source_target_pairs={{0,4},{1,5},{2,6},{3,7},{4,0},{5,1},{6,2},{7,3},{8,12},{9,13},{10,... | collective-permute-start | bytes 393224 | tf_op jit(solution)/shard_map/ppermute | solution.py:121
  32.8 3.3 %collective-permute-done.refs_2_ = bf16[1,512,128]{2,1,0:T(8,128)(2,1)S(1)} collective-permute-done((bf16[1,512,128]{2,1,0:T(8,128)(2,1)S(1)}, bf16[1,512,128]{2,1,0:T(8,128)(2,1)S(1)}, u32[]{:S(2)}, u32[]{:S(2)}) %collective-permute-start) | collective-permute-done | bytes 131104 | tf_op jit(solution)/shard_map/ppermute | solution.py:121
  36.2 7.4 %collective-permute-start.1 = (bf16[2,512,128]{2,1,0:T(8,128)(2,1)S(1)}, bf16[2,512,128]{2,1,0:T(8,128)(2,1)S(1)}, u32[]{:S(2)}, u32[]{:S(2)}) collective-permute-start(bf16[2,512,128]{2,1,0:T(8,128)(2,1)S(1)} %pad_maximum_fusion.1), channel_id=1, source_target_pairs={{0,2},{1,3},{2,0},{3,1},{4,6},{5,7},{6,4},{7,5},{8,10},{9,11},{10,... | collective-permute-start | bytes 786440 | tf_op jit(solution)/shard_map/ppermute | solution.py:121
  43.6 9.5 %collective-permute-done.1.refs_3_ = bf16[2,512,128]{2,1,0:T(8,128)(2,1)S(1)} collective-permute-done((bf16[2,512,128]{2,1,0:T(8,128)(2,1)S(1)}, bf16[2,512,128]{2,1,0:T(8,128)(2,1)S(1)}, u32[]{:S(2)}, u32[]{:S(2)}) %collective-permute-start.1) | collective-permute-done | bytes 262176 | tf_op jit(solution)/shard_map/ppermute | solution.py:121
  54.0 1.9 %collective-permute-start.2 = (bf16[4,512,128]{2,1,0:T(8,128)(2,1)}, bf16[4,512,128]{2,1,0:T(8,128)(2,1)S(1)}, u32[]{:S(2)}, u32[]{:S(2)}) collective-permute-start(bf16[4,512,128]{2,1,0:T(8,128)(2,1)} %pad_maximum_fusion), channel_id=1, source_target_pairs={{0,1},{1,0},{2,3},{3,2},{4,5},{5,4},{6,7},{7,6},{8,9},{9,8},{10,11... | collective-permute-start | bytes 1572872 | tf_op jit(solution)/shard_map/ppermute | solution.py:121
  56.9 11.8 %collective-permute-done.2.refs_4_ = bf16[4,512,128]{2,1,0:T(8,128)(2,1)S(1)} collective-permute-done((bf16[4,512,128]{2,1,0:T(8,128)(2,1)}, bf16[4,512,128]{2,1,0:T(8,128)(2,1)S(1)}, u32[]{:S(2)}, u32[]{:S(2)}) %collective-permute-start.2) | collective-permute-done | bytes 524320 | tf_op jit(solution)/shard_map/ppermute | solution.py:121
  71.8 3.6 %collective-permute-start.3 = (bf16[1024,512]{1,0:T(8,128)(2,1)S(1)}, bf16[1024,512]{1,0:T(8,128)(2,1)}, u32[]{:S(2)}, u32[]{:S(2)}) collective-permute-start(bf16[1024,512]{1,0:T(8,128)(2,1)S(1)} %flip.1.fa_ref), channel_id=1, source_target_pairs={{0,8},{8,0},{1,9},{9,1},{2,10},{10,2},{3,11},{11,3},{4,12},{12,4},... | collective-permute-start | bytes 3145736 | tf_op jit(solution)/shard_map/ppermute | solution.py:300
  77.4 1.3 merge_tiles.1
  78.7 3.3 %collective-permute-start.4 = (bf16[512,512]{1,0:T(8,128)(2,1)S(1)}, bf16[512,512]{1,0:T(8,128)(2,1)S(1)}, u32[]{:S(2)}, u32[]{:S(2)}) collective-permute-start(bf16[512,512]{1,0:T(8,128)(2,1)S(1)} %get-tuple-element.15.give_ref), channel_id=1, source_target_pairs={{0,8},{8,0},{1,9},{9,1},{2,10},{10,2},{3,11},{11,3},{4,12},{12,4},... | collective-permute-start | bytes 1572872 | tf_op jit(solution)/shard_map/ppermute | solution.py:312
  83.6 2.7 %weight_terms.1 = bf16[4,1024,128]{2,1,0:T(8,128)(2,1)S(1)} custom-call(bf16[1024,512]{1,0:T(8,128)(2,1)S(1)} %flip.1.fa_ref, bf16[1024,512]{1,0:T(8,128)(2,1)} %collective-permute-done.3.fb_ref, bf16[512,512]{1,0:T(8,128)(2,1)S(1)} %get-tuple-element.14.ga_ref.keep_ref, bf16[512,512]{1,0:T(8,128)(2,1)S(1)} %collective-permute-done.4.gb_ref), custom_call_target="tpu_custom_call" | custom-call | flops 1073741824 | bytes 4194304 | tf_op jit(solution)/shard_map/weight_terms/pallas_call | solution.py:205
  86.3 21.5 %all_to_all.25.in_ref = bf16[4,1024,128]{2,1,0:T(8,128)(2,1)S(1)} all-to-all(bf16[4,1024,128]{2,1,0:T(8,128)(2,1)S(1)} %weight_terms.1), channel_id=1, replica_groups=mesh['z'=8,'x'=4,'core'=2,'y'=8] {'x'}, dimensions={0} | all-to-all | bytes 2097152 | tf_op jit(solution)/shard_map/all_to_all | solution.py:258
  108.7 5.7 %all-to-all-start.2 = ((bf16[8,128,128]{2,1,0:T(8,128)(2,1)}), bf16[8,128,128]{2,1,0:T(8,128)(2,1)S(1)}, u32[]{:S(2)}, u32[]{:S(2)}) async-start(bf16[8,128,128]{2,1,0:T(8,128)(2,1)} %bitcast.10), calls=%async_computation.3 | async-start | bytes 524288 | tf_op jit(solution)/shard_map/all_to_all | solution.py:258
  114.4 1.3 all-gather.3.cloned.1.call-done
  116.8 1.6 copy-done.9
  118.4 3.3 %feature_terms.1 = (f32[8,512,128]{2,1,0:T(8,128)}, f32[8,128]{1,0:T(8,128)S(1)}) custom-call(s32[1]{0:T(128)} %bitcast.core_ref.at_ref, bf16[512,512]{1,0:T(8,128)(2,1)S(1)} %copy-done.7, bf16[512,512]{1,0:T(8,128)(2,1)S(1)} %copy-done.11, bf16[64,8,16,128]{3,2,1,0:T(8,128)(2,1)S(1)} %bitcast.26), custom_call_target="tpu_custom_call" | custom-call | flops 1073741824 | bytes 4194304 | tf_op jit(solution)/shard_map/feature_terms/pallas_call | solution.py:236
  121.7 3.0 %all-to-all-done.2.in_ref = bf16[8,128,128]{2,1,0:T(8,128)(2,1)S(1)} async-done(((bf16[8,128,128]{2,1,0:T(8,128)(2,1)}), bf16[8,128,128]{2,1,0:T(8,128)(2,1)S(1)}, u32[]{:S(2)}, u32[]{:S(2)}) %all-to-all-start.2) | async-done | bytes 262176 | tf_op jit(solution)/shard_map/all_to_all | solution.py:258
  124.8 12.1 %all_to_all.26 = bf16[8,128,128]{2,1,0:T(8,128)(2,1)S(1)} all-to-all(bf16[8,128,128]{2,1,0:T(8,128)(2,1)S(1)} %fold.3), channel_id=1, replica_groups=mesh['z'=8,'x'=4,'core'=2,'y'=8] {'z'}, dimensions={0} | all-to-all | bytes 524288 | tf_op jit(solution)/shard_map/all_to_all | solution.py:258
  138.0 3.5 %all-to-all-start.4 = ((bf16[4,1024,128]{2,1,0:T(8,128)(2,1)}), bf16[4,1024,128]{2,1,0:T(8,128)(2,1)S(1)}, u32[]{:S(2)}, u32[]{:S(2)}) async-start(bf16[4,1024,128]{2,1,0:T(8,128)(2,1)} %broadcast_in_dim.76), calls=%async_computation.5 | async-start | bytes 2097152 | tf_op jit(solution)/shard_map/all_to_all | solution.py:258
  141.5 11.5 %all-to-all-done.4 = bf16[4,1024,128]{2,1,0:T(8,128)(2,1)S(1)} async-done(((bf16[4,1024,128]{2,1,0:T(8,128)(2,1)}), bf16[4,1024,128]{2,1,0:T(8,128)(2,1)S(1)}, u32[]{:S(2)}, u32[]{:S(2)}) %all-to-all-start.4) | async-done | bytes 1048608 | tf_op jit(solution)/shard_map/all_to_all | solution.py:258
  153.0 6.5 %collective-permute-start.5 = (bf16[4096,128]{1,0:T(8,128)(2,1)S(1)}, bf16[4096,128]{1,0:T(8,128)(2,1)S(1)}, u32[]{:S(2)}, u32[]{:S(2)}) collective-permute-start(bf16[4096,128]{1,0:T(8,128)(2,1)S(1)} %bitcast.24), channel_id=1, source_target_pairs={{0,8},{8,0},{1,9},{9,1},{2,10},{10,2},{3,11},{11,3},{4,12},{12,4},... | collective-permute-start | bytes 3145736 | tf_op jit(solution)/shard_map/ppermute | solution.py:324
  160.4 1.3 collective-permute-done.5.part_ref
  162.7 1.6 fusion
  (55 shorter events, 13.5 us)
Async XLA Ops:
  9.5 15.8 %copy-start = (bf16[512,128]{1,0:T(8,128)(2,1)S(1)}, bf16[512,128]{1,0:T(8,128)(2,1)}, u32[]{:S(2)}) copy-start(bf16[512,128]{1,0:T(8,128)(2,1)} %param.11) | copy-start | bytes 393220
  9.5 46.4 %copy-start.14 = (s32[512]{0:T(512)S(1)}, s32[512]{0:T(512)}, u32[]{:S(2)}) copy-start(s32[512]{0:T(512)} %param.13) | copy-start | bytes 6148
  9.5 46.4 %copy-start.15 = (f32[3,128]{1,0:T(4,128)S(1)}, f32[3,128]{1,0:T(4,128)}, u32[]{:S(2)}) copy-start(f32[3,128]{1,0:T(4,128)} %param.14) | copy-start | bytes 4612
  9.5 46.4 %copy-start.13 = (bf16[512,128]{1,0:T(8,128)(2,1)S(1)}, bf16[512,128]{1,0:T(8,128)(2,1)}, u32[]{:S(2)}) copy-start(bf16[512,128]{1,0:T(8,128)(2,1)} %param.12) | copy-start | bytes 393220
  9.6 66.6 %all-to-all-start = ((bf16[64,128,128]{2,1,0:T(8,128)(2,1)}), bf16[64,128,128]{2,1,0:T(8,128)(2,1)S(1)}, u32[]{:S(2)}, u32[]{:S(2)}) async-start(bf16[64,128,128]{2,1,0:T(8,128)(2,1)} %pick_blocks.1), calls=%async_computation | async-start | bytes 4194304 | tf_op jit(solution)/shard_map/all_to_all | solution.py:258
  24.5 51.6 %copy-start.16 = (s32[32]{0:T(128)S(1)}, s32[32]{0:T(128)}, u32[]{:S(2)}) copy-start(s32[32]{0:T(128)} %param.18) | copy-start | bytes 388
  24.5 51.6 %copy-start.17 = (s32[32]{0:T(128)S(1)}, s32[32]{0:T(128)}, u32[]{:S(2)}) copy-start(s32[32]{0:T(128)} %param.17) | copy-start | bytes 388
  24.6 51.6 %copy-start.8 = (s32[32]{0:T(128)S(1)}, s32[32]{0:T(128)}, u32[]{:S(2)}) copy-start(s32[32]{0:T(128)} %peer_ref.1) | copy-start | bytes 388
  24.6 91.2 %all-gather.3.cloned.1.call-start = ((), (), s32[]{:S(2)}) async-start(), calls=%async_computation.7 | async-start | bytes 2129920 | tf_op jit(solution)/shard_map/all_gather | solution.py:291
  25.3 10.8 %collective-permute-start = (bf16[1,512,128]{2,1,0:T(8,128)(2,1)S(1)}, bf16[1,512,128]{2,1,0:T(8,128)(2,1)S(1)}, u32[]{:S(2)}, u32[]{:S(2)}) collective-permute-start(bf16[1,512,128]{2,1,0:T(8,128)(2,1)S(1)} %bitcast.20), channel_id=1, source_target_pairs={{0,4},{1,5},{2,6},{3,7},{4,0},{5,1},{6,2},{7,3},{8,12},{9,13},{10,... | collective-permute-start | bytes 393224 | tf_op jit(solution)/shard_map/ppermute | solution.py:121
  36.2 16.9 %collective-permute-start.1 = (bf16[2,512,128]{2,1,0:T(8,128)(2,1)S(1)}, bf16[2,512,128]{2,1,0:T(8,128)(2,1)S(1)}, u32[]{:S(2)}, u32[]{:S(2)}) collective-permute-start(bf16[2,512,128]{2,1,0:T(8,128)(2,1)S(1)} %pad_maximum_fusion.1), channel_id=1, source_target_pairs={{0,2},{1,3},{2,0},{3,1},{4,6},{5,7},{6,4},{7,5},{8,10},{9,11},{10,... | collective-permute-start | bytes 786440 | tf_op jit(solution)/shard_map/ppermute | solution.py:121
  53.1 15.6 %copy-start.1 = (bf16[2,512,128]{2,1,0:T(8,128)(2,1)}, bf16[2,512,128]{2,1,0:T(8,128)(2,1)S(1)}, u32[]{:S(2)}) copy-start(bf16[2,512,128]{2,1,0:T(8,128)(2,1)S(1)} %collective-permute-done.1.refs_3_) | copy-start | bytes 786436
  54.0 14.7 %collective-permute-start.2 = (bf16[4,512,128]{2,1,0:T(8,128)(2,1)}, bf16[4,512,128]{2,1,0:T(8,128)(2,1)S(1)}, u32[]{:S(2)}, u32[]{:S(2)}) collective-permute-start(bf16[4,512,128]{2,1,0:T(8,128)(2,1)} %pad_maximum_fusion), channel_id=1, source_target_pairs={{0,1},{1,0},{2,3},{3,2},{4,5},{5,4},{6,7},{7,6},{8,9},{9,8},{10,11... | collective-permute-start | bytes 1572872 | tf_op jit(solution)/shard_map/ppermute | solution.py:121
  71.8 11.0 %collective-permute-start.3 = (bf16[1024,512]{1,0:T(8,128)(2,1)S(1)}, bf16[1024,512]{1,0:T(8,128)(2,1)}, u32[]{:S(2)}, u32[]{:S(2)}) collective-permute-start(bf16[1024,512]{1,0:T(8,128)(2,1)S(1)} %flip.1.fa_ref), channel_id=1, source_target_pairs={{0,8},{8,0},{1,9},{9,1},{2,10},{10,2},{3,11},{11,3},{4,12},{12,4},... | collective-permute-start | bytes 3145736 | tf_op jit(solution)/shard_map/ppermute | solution.py:300
  76.2 1.2 copy-start.3
  78.7 7.6 %copy-start.6 = (bf16[512,512]{1,0:T(8,128)(2,1)}, bf16[512,512]{1,0:T(8,128)(2,1)S(1)}, u32[]{:S(2)}) copy-start(bf16[512,512]{1,0:T(8,128)(2,1)S(1)} %get-tuple-element.14.ga_ref.keep_ref) | copy-start | bytes 1572868
  78.7 4.9 %collective-permute-start.4 = (bf16[512,512]{1,0:T(8,128)(2,1)S(1)}, bf16[512,512]{1,0:T(8,128)(2,1)S(1)}, u32[]{:S(2)}, u32[]{:S(2)}) collective-permute-start(bf16[512,512]{1,0:T(8,128)(2,1)S(1)} %get-tuple-element.15.give_ref), channel_id=1, source_target_pairs={{0,8},{8,0},{1,9},{9,1},{2,10},{10,2},{3,11},{11,3},{4,12},{12,4},... | collective-permute-start | bytes 1572872 | tf_op jit(solution)/shard_map/ppermute | solution.py:312
  86.3 29.5 %copy-start.11 = (bf16[512,512]{1,0:T(8,128)(2,1)S(1)}, bf16[512,512]{1,0:T(8,128)(2,1)}, u32[]{:S(2)}) copy-start(bf16[512,512]{1,0:T(8,128)(2,1)} %copy-done.10) | copy-start | bytes 1572868
  108.7 16.1 %all-to-all-start.2 = ((bf16[8,128,128]{2,1,0:T(8,128)(2,1)}), bf16[8,128,128]{2,1,0:T(8,128)(2,1)S(1)}, u32[]{:S(2)}, u32[]{:S(2)}) async-start(bf16[8,128,128]{2,1,0:T(8,128)(2,1)} %bitcast.10), calls=%async_computation.3 | async-start | bytes 524288 | tf_op jit(solution)/shard_map/all_to_all | solution.py:258
  114.4 48.3 %reduce-scatter.2.cloned.1.call-start = ((), (), s32[]{:S(2)}) async-start(), calls=%async_computation.6 | async-start | bytes 2359296 | tf_op jit(solution)/shard_map/reduce_scatter | solution.py:319
  116.8 1.6 copy-start.9
  138.0 15.0 %all-to-all-start.4 = ((bf16[4,1024,128]{2,1,0:T(8,128)(2,1)}), bf16[4,1024,128]{2,1,0:T(8,128)(2,1)S(1)}, u32[]{:S(2)}, u32[]{:S(2)}) async-start(bf16[4,1024,128]{2,1,0:T(8,128)(2,1)} %broadcast_in_dim.76), calls=%async_computation.5 | async-start | bytes 2097152 | tf_op jit(solution)/shard_map/all_to_all | solution.py:258
  153.0 8.7 %collective-permute-start.5 = (bf16[4096,128]{1,0:T(8,128)(2,1)S(1)}, bf16[4096,128]{1,0:T(8,128)(2,1)S(1)}, u32[]{:S(2)}, u32[]{:S(2)}) collective-permute-start(bf16[4096,128]{1,0:T(8,128)(2,1)S(1)} %bitcast.24), channel_id=1, source_target_pairs={{0,8},{8,0},{1,9},{9,1},{2,10},{10,2},{3,11},{11,3},{4,12},{12,4},... | collective-permute-start | bytes 3145736 | tf_op jit(solution)/shard_map/ppermute | solution.py:324
  160.4 2.3 %copy-start.12 = (f32[512,128]{1,0:T(8,128)S(1)}, f32[512,128]{1,0:T(8,128)}, u32[]{:S(2)}) copy-start(f32[512,128]{1,0:T(8,128)} %select_multiply_fusion) | copy-start | bytes 786436
  (5 other events, 4.6 us)
Sparse Core Ops, SparseCore 0:
  28.8 86.9 all-gather.2
  121.8 38.9 reduce-scatter.1

commit v5 on v4

--- a/solution.py
+++ b/solution.py
@@ -248,7 +248,6 @@
             pl.BlockSpec((8, 128), lambda c: (0, 0)),
         ),
         scratch_shapes=[pltpu.VMEM((group * jw, 2 * wide), BF)],
-        compiler_params=pltpu.CompilerParams(vmem_limit_bytes=12 << 20),
         cost_estimate=cost(4 * n * jw * rows * wide, 4 << 20),
         name="feature_terms",
     )(core, keep, give, shards)

time: 173 us -> 173 us (level)
  local copies, waits for them, and re-layouts: 8.6 us -> 5.19 us
  Pallas kernels: 12.8 us -> 14.7 us
    unnamed x36 -> x32, local copies, waits for them, and re-layouts: 7.49 us -> 4.08 us
    pallas_call x1, Pallas kernels: 3.29 us -> 5.17 us  [feature_terms(): pl.pallas_call(kernel, out_shape=(jax.ShapeDtypeStruct((n, rows, jw), F32...]
  transfers between devices with their start and end apart: 11 -> 11, of which waited for: 8 -> 8; matrix products, arithmetic and copies ran while one was open for 2% -> 2% of each run, Pallas kernels for 6% -> 7%
where the time goes in v5:
time: 173 us; the launch traced here: 171 us
  starting transfers between devices  54.6 us (32%)
  waiting for transfers between devices  44.5 us (26%)
  blocking collectives  33.5 us (19%)
  between operations  15 us (9%)
  Pallas kernels  14.7 us (8%)
  local copies, waits for them, and re-layouts  5.19 us (3%)
  other arithmetic  3.46 us (2%)
    all_to_all x2, blocking collectives, exchange(): return lax.all_to_all(parts, axis, split_axis=0, concat_axis=0, tiled=True)  33.5 us
    ppermute x3, waiting for transfers between devices, double(): got = lax.ppermute(held, axis, [(i, i ^ step) for i in range(n)])  24.7 us
    all_to_all x3, starting transfers between devices, exchange(): return lax.all_to_all(parts, axis, split_axis=0, concat_axis=0, tiled=True)  24.2 us
    ppermute x3, starting transfers between devices, double(): got = lax.ppermute(held, axis, [(i, i ^ step) for i in range(n)])  16.8 us
    all_to_all x3, waiting for transfers between devices, exchange(): return lax.all_to_all(parts, axis, split_axis=0, concat_axis=0, tiled=True)  14.9 us
    ppermute x1, starting transfers between devices, body(): lax.ppermute(mine, 'core', swap)  6.56 us
    pallas_call x1, Pallas kernels, feature_terms(): pl.pallas_call(kernel, out_shape=(jax.ShapeDtypeStruct((n, rows, jw), F32...  5.17 us
    unnamed x32, local copies, waits for them, and re-layouts  4.08 us
  transfers between devices with their start and end apart: 11, of which 8 were waited for; matrix products, arithmetic and copies ran while one was open for 2% of the time, Pallas kernels for 7%

profile of v5, /device:TPU:1, one launch (start us, length us, event | category | flops | bytes accessed | tf_op | source)
XLA Modules:
  0.0 171.0 jit_solution(18186252305700498327)
XLA Ops:
  7.2 2.4 %pick_blocks.1 = bf16[64,128,128]{2,1,0:T(8,128)(2,1)} custom-call(s32[64]{0:T(128)} %bitcast.28, bf16[4,128,128]{2,1,0:T(8,128)(2,1)} %bitcast.27), custom_call_target="tpu_custom_call" | custom-call | bytes 2097152 | tf_op jit(solution)/shard_map/pick_blocks/pallas_call | solution.py:32
  9.6 15.0 %all-to-all-start = ((bf16[64,128,128]{2,1,0:T(8,128)(2,1)}), bf16[64,128,128]{2,1,0:T(8,128)(2,1)S(1)}, u32[]{:S(2)}, u32[]{:S(2)}) async-start(bf16[64,128,128]{2,1,0:T(8,128)(2,1)} %pick_blocks.1), calls=%async_computation | async-start | bytes 4194304 | tf_op jit(solution)/shard_map/all_to_all | solution.py:257
  25.3 7.5 %collective-permute-start = (bf16[1,512,128]{2,1,0:T(8,128)(2,1)S(1)}, bf16[1,512,128]{2,1,0:T(8,128)(2,1)S(1)}, u32[]{:S(2)}, u32[]{:S(2)}) collective-permute-start(bf16[1,512,128]{2,1,0:T(8,128)(2,1)S(1)} %bitcast.20), channel_id=1, source_target_pairs={{0,4},{1,5},{2,6},{3,7},{4,0},{5,1},{6,2},{7,3},{8,12},{9,13},{10,... | collective-permute-start | bytes 393224 | tf_op jit(solution)/shard_map/ppermute | solution.py:121
  32.8 3.3 %collective-permute-done.refs_2_ = bf16[1,512,128]{2,1,0:T(8,128)(2,1)S(1)} collective-permute-done((bf16[1,512,128]{2,1,0:T(8,128)(2,1)S(1)}, bf16[1,512,128]{2,1,0:T(8,128)(2,1)S(1)}, u32[]{:S(2)}, u32[]{:S(2)}) %collective-permute-start) | collective-permute-done | bytes 131104 | tf_op jit(solution)/shard_map/ppermute | solution.py:121
  36.2 7.4 %collective-permute-start.1 = (bf16[2,512,128]{2,1,0:T(8,128)(2,1)S(1)}, bf16[2,512,128]{2,1,0:T(8,128)(2,1)S(1)}, u32[]{:S(2)}, u32[]{:S(2)}) collective-permute-start(bf16[2,512,128]{2,1,0:T(8,128)(2,1)S(1)} %pad_maximum_fusion.1), channel_id=1, source_target_pairs={{0,2},{1,3},{2,0},{3,1},{4,6},{5,7},{6,4},{7,5},{8,10},{9,11},{10,... | collective-permute-start | bytes 786440 | tf_op jit(solution)/shard_map/ppermute | solution.py:121
  43.6 9.5 %collective-permute-done.1.refs_3_ = bf16[2,512,128]{2,1,0:T(8,128)(2,1)S(1)} collective-permute-done((bf16[2,512,128]{2,1,0:T(8,128)(2,1)S(1)}, bf16[2,512,128]{2,1,0:T(8,128)(2,1)S(1)}, u32[]{:S(2)}, u32[]{:S(2)}) %collective-permute-start.1) | collective-permute-done | bytes 262176 | tf_op jit(solution)/shard_map/ppermute | solution.py:121
  54.0 1.9 %collective-permute-start.2 = (bf16[4,512,128]{2,1,0:T(8,128)(2,1)}, bf16[4,512,128]{2,1,0:T(8,128)(2,1)S(1)}, u32[]{:S(2)}, u32[]{:S(2)}) collective-permute-start(bf16[4,512,128]{2,1,0:T(8,128)(2,1)} %pad_maximum_fusion), channel_id=1, source_target_pairs={{0,1},{1,0},{2,3},{3,2},{4,5},{5,4},{6,7},{7,6},{8,9},{9,8},{10,11... | collective-permute-start | bytes 1572872 | tf_op jit(solution)/shard_map/ppermute | solution.py:121
  56.8 11.8 %collective-permute-done.2.refs_4_ = bf16[4,512,128]{2,1,0:T(8,128)(2,1)S(1)} collective-permute-done((bf16[4,512,128]{2,1,0:T(8,128)(2,1)}, bf16[4,512,128]{2,1,0:T(8,128)(2,1)S(1)}, u32[]{:S(2)}, u32[]{:S(2)}) %collective-permute-start.2) | collective-permute-done | bytes 524320 | tf_op jit(solution)/shard_map/ppermute | solution.py:121
  71.8 3.6 %collective-permute-start.3 = (bf16[1024,512]{1,0:T(8,128)(2,1)S(1)}, bf16[1024,512]{1,0:T(8,128)(2,1)}, u32[]{:S(2)}, u32[]{:S(2)}) collective-permute-start(bf16[1024,512]{1,0:T(8,128)(2,1)S(1)} %flip.1.fa_ref), channel_id=1, source_target_pairs={{0,8},{8,0},{1,9},{9,1},{2,10},{10,2},{3,11},{11,3},{4,12},{12,4},... | collective-permute-start | bytes 3145736 | tf_op jit(solution)/shard_map/ppermute | solution.py:299
  77.4 1.3 merge_tiles.1
  78.7 3.3 %collective-permute-start.4 = (bf16[512,512]{1,0:T(8,128)(2,1)S(1)}, bf16[512,512]{1,0:T(8,128)(2,1)S(1)}, u32[]{:S(2)}, u32[]{:S(2)}) collective-permute-start(bf16[512,512]{1,0:T(8,128)(2,1)S(1)} %get-tuple-element.15.give_ref), channel_id=1, source_target_pairs={{0,8},{8,0},{1,9},{9,1},{2,10},{10,2},{3,11},{11,3},{4,12},{12,4},... | collective-permute-start | bytes 1572872 | tf_op jit(solution)/shard_map/ppermute | solution.py:311
  82.1 1.5 collective-permute-done.4.gb_ref
  83.6 2.7 %weight_terms.1 = bf16[4,1024,128]{2,1,0:T(8,128)(2,1)S(1)} custom-call(bf16[1024,512]{1,0:T(8,128)(2,1)S(1)} %flip.1.fa_ref, bf16[1024,512]{1,0:T(8,128)(2,1)} %collective-permute-done.3.fb_ref, bf16[512,512]{1,0:T(8,128)(2,1)S(1)} %get-tuple-element.14.ga_ref.keep_ref, bf16[512,512]{1,0:T(8,128)(2,1)S(1)} %collective-permute-done.4.gb_ref), custom_call_target="tpu_custom_call" | custom-call | flops 1073741824 | bytes 4194304 | tf_op jit(solution)/shard_map/weight_terms/pallas_call | solution.py:205
  86.3 21.4 %all_to_all.25.in_ref = bf16[4,1024,128]{2,1,0:T(8,128)(2,1)S(1)} all-to-all(bf16[4,1024,128]{2,1,0:T(8,128)(2,1)S(1)} %weight_terms.1), channel_id=1, replica_groups=mesh['z'=8,'x'=4,'core'=2,'y'=8] {'x'}, dimensions={0} | all-to-all | bytes 2097152 | tf_op jit(solution)/shard_map/all_to_all | solution.py:257
  108.6 5.7 %all-to-all-start.2 = ((bf16[8,128,128]{2,1,0:T(8,128)(2,1)}), bf16[8,128,128]{2,1,0:T(8,128)(2,1)S(1)}, u32[]{:S(2)}, u32[]{:S(2)}) async-start(bf16[8,128,128]{2,1,0:T(8,128)(2,1)} %bitcast.10), calls=%async_computation.3 | async-start | bytes 524288 | tf_op jit(solution)/shard_map/all_to_all | solution.py:257
  114.4 1.4 all-gather.3.cloned.1.call-done
  115.8 5.2 %feature_terms.1 = (f32[8,512,128]{2,1,0:T(8,128)}, f32[8,128]{1,0:T(8,128)}) custom-call(s32[1]{0:T(128)} %bitcast.core_ref.at_ref, bf16[512,512]{1,0:T(8,128)(2,1)} %copy-done.6, bf16[512,512]{1,0:T(8,128)(2,1)} %copy-done.9, bf16[64,8,16,128]{3,2,1,0:T(8,128)(2,1)} %bitcast.29), custom_call_target="tpu_custom_call" | custom-call | flops 1073741824 | bytes 4194304 | tf_op jit(solution)/shard_map/feature_terms/pallas_call | solution.py:236
  120.9 3.6 %all-to-all-done.2.in_ref = bf16[8,128,128]{2,1,0:T(8,128)(2,1)S(1)} async-done(((bf16[8,128,128]{2,1,0:T(8,128)(2,1)}), bf16[8,128,128]{2,1,0:T(8,128)(2,1)S(1)}, u32[]{:S(2)}, u32[]{:S(2)}) %all-to-all-start.2) | async-done | bytes 262176 | tf_op jit(solution)/shard_map/all_to_all | solution.py:257
  124.6 12.1 %all_to_all.26 = bf16[8,128,128]{2,1,0:T(8,128)(2,1)S(1)} all-to-all(bf16[8,128,128]{2,1,0:T(8,128)(2,1)S(1)} %fold.3), channel_id=1, replica_groups=mesh['z'=8,'x'=4,'core'=2,'y'=8] {'z'}, dimensions={0} | all-to-all | bytes 524288 | tf_op jit(solution)/shard_map/all_to_all | solution.py:257
  137.8 3.5 %all-to-all-start.4 = ((bf16[4,1024,128]{2,1,0:T(8,128)(2,1)}), bf16[4,1024,128]{2,1,0:T(8,128)(2,1)S(1)}, u32[]{:S(2)}, u32[]{:S(2)}) async-start(bf16[4,1024,128]{2,1,0:T(8,128)(2,1)} %broadcast_in_dim.76), calls=%async_computation.5 | async-start | bytes 2097152 | tf_op jit(solution)/shard_map/all_to_all | solution.py:257
  141.3 11.4 %all-to-all-done.4 = bf16[4,1024,128]{2,1,0:T(8,128)(2,1)S(1)} async-done(((bf16[4,1024,128]{2,1,0:T(8,128)(2,1)}), bf16[4,1024,128]{2,1,0:T(8,128)(2,1)S(1)}, u32[]{:S(2)}, u32[]{:S(2)}) %all-to-all-start.4) | async-done | bytes 1048608 | tf_op jit(solution)/shard_map/all_to_all | solution.py:257
  152.7 6.6 %collective-permute-start.5 = (bf16[4096,128]{1,0:T(8,128)(2,1)S(1)}, bf16[4096,128]{1,0:T(8,128)(2,1)S(1)}, u32[]{:S(2)}, u32[]{:S(2)}) collective-permute-start(bf16[4096,128]{1,0:T(8,128)(2,1)S(1)} %bitcast.24), channel_id=1, source_target_pairs={{0,8},{8,0},{1,9},{9,1},{2,10},{10,2},{3,11},{11,3},{4,12},{12,4},... | collective-permute-start | bytes 3145736 | tf_op jit(solution)/shard_map/ppermute | solution.py:323
  160.2 1.3 collective-permute-done.5.part_ref
  162.5 1.6 fusion
  (51 shorter events, 11.0 us)
Async XLA Ops:
  9.5 15.8 %copy-start = (bf16[512,128]{1,0:T(8,128)(2,1)S(1)}, bf16[512,128]{1,0:T(8,128)(2,1)}, u32[]{:S(2)}) copy-start(bf16[512,128]{1,0:T(8,128)(2,1)} %param.11) | copy-start | bytes 393220
  9.5 46.4 %copy-start.12 = (s32[512]{0:T(512)S(1)}, s32[512]{0:T(512)}, u32[]{:S(2)}) copy-start(s32[512]{0:T(512)} %param.13) | copy-start | bytes 6148
  9.5 46.4 %copy-start.13 = (f32[3,128]{1,0:T(4,128)S(1)}, f32[3,128]{1,0:T(4,128)}, u32[]{:S(2)}) copy-start(f32[3,128]{1,0:T(4,128)} %param.14) | copy-start | bytes 4612
  9.5 46.4 %copy-start.11 = (bf16[512,128]{1,0:T(8,128)(2,1)S(1)}, bf16[512,128]{1,0:T(8,128)(2,1)}, u32[]{:S(2)}) copy-start(bf16[512,128]{1,0:T(8,128)(2,1)} %param.12) | copy-start | bytes 393220
  9.6 66.6 %all-to-all-start = ((bf16[64,128,128]{2,1,0:T(8,128)(2,1)}), bf16[64,128,128]{2,1,0:T(8,128)(2,1)S(1)}, u32[]{:S(2)}, u32[]{:S(2)}) async-start(bf16[64,128,128]{2,1,0:T(8,128)(2,1)} %pick_blocks.1), calls=%async_computation | async-start | bytes 4194304 | tf_op jit(solution)/shard_map/all_to_all | solution.py:257
  24.5 51.6 %copy-start.14 = (s32[32]{0:T(128)S(1)}, s32[32]{0:T(128)}, u32[]{:S(2)}) copy-start(s32[32]{0:T(128)} %param.18) | copy-start | bytes 388
  24.6 51.6 %copy-start.15 = (s32[32]{0:T(128)S(1)}, s32[32]{0:T(128)}, u32[]{:S(2)}) copy-start(s32[32]{0:T(128)} %param.17) | copy-start | bytes 388
  24.6 51.6 %copy-start.8 = (s32[32]{0:T(128)S(1)}, s32[32]{0:T(128)}, u32[]{:S(2)}) copy-start(s32[32]{0:T(128)} %peer_ref.1) | copy-start | bytes 388
  24.6 91.2 %all-gather.3.cloned.1.call-start = ((), (), s32[]{:S(2)}) async-start(), calls=%async_computation.7 | async-start | bytes 2129920 | tf_op jit(solution)/shard_map/all_gather | solution.py:290
  25.3 10.8 %collective-permute-start = (bf16[1,512,128]{2,1,0:T(8,128)(2,1)S(1)}, bf16[1,512,128]{2,1,0:T(8,128)(2,1)S(1)}, u32[]{:S(2)}, u32[]{:S(2)}) collective-permute-start(bf16[1,512,128]{2,1,0:T(8,128)(2,1)S(1)} %bitcast.20), channel_id=1, source_target_pairs={{0,4},{1,5},{2,6},{3,7},{4,0},{5,1},{6,2},{7,3},{8,12},{9,13},{10,... | collective-permute-start | bytes 393224 | tf_op jit(solution)/shard_map/ppermute | solution.py:121
  36.2 16.9 %collective-permute-start.1 = (bf16[2,512,128]{2,1,0:T(8,128)(2,1)S(1)}, bf16[2,512,128]{2,1,0:T(8,128)(2,1)S(1)}, u32[]{:S(2)}, u32[]{:S(2)}) collective-permute-start(bf16[2,512,128]{2,1,0:T(8,128)(2,1)S(1)} %pad_maximum_fusion.1), channel_id=1, source_target_pairs={{0,2},{1,3},{2,0},{3,1},{4,6},{5,7},{6,4},{7,5},{8,10},{9,11},{10,... | collective-permute-start | bytes 786440 | tf_op jit(solution)/shard_map/ppermute | solution.py:121
  53.1 15.6 %copy-start.1 = (bf16[2,512,128]{2,1,0:T(8,128)(2,1)}, bf16[2,512,128]{2,1,0:T(8,128)(2,1)S(1)}, u32[]{:S(2)}) copy-start(bf16[2,512,128]{2,1,0:T(8,128)(2,1)S(1)} %collective-permute-done.1.refs_3_) | copy-start | bytes 786436
  54.0 14.7 %collective-permute-start.2 = (bf16[4,512,128]{2,1,0:T(8,128)(2,1)}, bf16[4,512,128]{2,1,0:T(8,128)(2,1)S(1)}, u32[]{:S(2)}, u32[]{:S(2)}) collective-permute-start(bf16[4,512,128]{2,1,0:T(8,128)(2,1)} %pad_maximum_fusion), channel_id=1, source_target_pairs={{0,1},{1,0},{2,3},{3,2},{4,5},{5,4},{6,7},{7,6},{8,9},{9,8},{10,11... | collective-permute-start | bytes 1572872 | tf_op jit(solution)/shard_map/ppermute | solution.py:121
  71.8 10.3 %collective-permute-start.3 = (bf16[1024,512]{1,0:T(8,128)(2,1)S(1)}, bf16[1024,512]{1,0:T(8,128)(2,1)}, u32[]{:S(2)}, u32[]{:S(2)}) collective-permute-start(bf16[1024,512]{1,0:T(8,128)(2,1)S(1)} %flip.1.fa_ref), channel_id=1, source_target_pairs={{0,8},{8,0},{1,9},{9,1},{2,10},{10,2},{3,11},{11,3},{4,12},{12,4},... | collective-permute-start | bytes 3145736 | tf_op jit(solution)/shard_map/ppermute | solution.py:299
  76.2 1.2 copy-start.3
  78.7 4.9 %copy-start.9 = (bf16[512,512]{1,0:T(8,128)(2,1)}, bf16[512,512]{1,0:T(8,128)(2,1)S(1)}, u32[]{:S(2)}) copy-start(bf16[512,512]{1,0:T(8,128)(2,1)S(1)} %get-tuple-element.15.give_ref) | copy-start | bytes 1572868
  78.7 7.6 %copy-start.6 = (bf16[512,512]{1,0:T(8,128)(2,1)}, bf16[512,512]{1,0:T(8,128)(2,1)S(1)}, u32[]{:S(2)}) copy-start(bf16[512,512]{1,0:T(8,128)(2,1)S(1)} %get-tuple-element.14.ga_ref.keep_ref) | copy-start | bytes 1572868
  78.7 4.9 %collective-permute-start.4 = (bf16[512,512]{1,0:T(8,128)(2,1)S(1)}, bf16[512,512]{1,0:T(8,128)(2,1)S(1)}, u32[]{:S(2)}, u32[]{:S(2)}) collective-permute-start(bf16[512,512]{1,0:T(8,128)(2,1)S(1)} %get-tuple-element.15.give_ref), channel_id=1, source_target_pairs={{0,8},{8,0},{1,9},{9,1},{2,10},{10,2},{3,11},{11,3},{4,12},{12,4},... | collective-permute-start | bytes 1572872 | tf_op jit(solution)/shard_map/ppermute | solution.py:311
  108.6 15.9 %all-to-all-start.2 = ((bf16[8,128,128]{2,1,0:T(8,128)(2,1)}), bf16[8,128,128]{2,1,0:T(8,128)(2,1)S(1)}, u32[]{:S(2)}, u32[]{:S(2)}) async-start(bf16[8,128,128]{2,1,0:T(8,128)(2,1)} %bitcast.10), calls=%async_computation.3 | async-start | bytes 524288 | tf_op jit(solution)/shard_map/all_to_all | solution.py:257
  114.3 48.2 %reduce-scatter.2.cloned.1.call-start = ((), (), s32[]{:S(2)}) async-start(), calls=%async_computation.6 | async-start | bytes 2359296 | tf_op jit(solution)/shard_map/reduce_scatter | solution.py:318
  120.9 3.6 %copy-start.7 = (f32[8,128]{1,0:T(8,128)S(1)}, f32[8,128]{1,0:T(8,128)}, u32[]{:S(2)}) copy-start(f32[8,128]{1,0:T(8,128)} %get-tuple-element.19.rest_0_) | copy-start | bytes 12292
  137.8 14.9 %all-to-all-start.4 = ((bf16[4,1024,128]{2,1,0:T(8,128)(2,1)}), bf16[4,1024,128]{2,1,0:T(8,128)(2,1)S(1)}, u32[]{:S(2)}, u32[]{:S(2)}) async-start(bf16[4,1024,128]{2,1,0:T(8,128)(2,1)} %broadcast_in_dim.76), calls=%async_computation.5 | async-start | bytes 2097152 | tf_op jit(solution)/shard_map/all_to_all | solution.py:257
  152.7 8.8 %collective-permute-start.5 = (bf16[4096,128]{1,0:T(8,128)(2,1)S(1)}, bf16[4096,128]{1,0:T(8,128)(2,1)S(1)}, u32[]{:S(2)}, u32[]{:S(2)}) collective-permute-start(bf16[4096,128]{1,0:T(8,128)(2,1)S(1)} %bitcast.24), channel_id=1, source_target_pairs={{0,8},{8,0},{1,9},{9,1},{2,10},{10,2},{3,11},{11,3},{4,12},{12,4},... | collective-permute-start | bytes 3145736 | tf_op jit(solution)/shard_map/ppermute | solution.py:323
  160.2 2.3 %copy-start.10 = (f32[512,128]{1,0:T(8,128)S(1)}, f32[512,128]{1,0:T(8,128)}, u32[]{:S(2)}) copy-start(f32[512,128]{1,0:T(8,128)} %select_multiply_fusion) | copy-start | bytes 786436
  (3 other events, 2.8 us)
Sparse Core Ops, SparseCore 0:
  28.8 86.9 all-gather.2
  121.1 38.9 reduce-scatter.1
